TPU v7x, 256 devices: a whole 4x4x8 slice. The times are simulated.
256 devices in a mesh: chan: 32 (over z, x_hi, core), row: 4 (over y), col: 2 (over x_lo).
Axes of the slice: x: 4 (x_hi: 2, x_lo: 2; x = x_hi * 2 + x_lo), y: 4, z: 8, core: 2. Of those that a mesh axis runs over, the one named last changes fastest.
Arguments:
- voltages: bfloat16 [1024, 262144], P('chan', ('row', 'col')), may hold values from -6 to 6
Outputs:
- visibilities: float32 [256, 2, 1024, 1024], P('chan', None, 'row', 'col')
All inputs are finite; a program needn't handle non-finite values.
Results may differ from a plain program's by a relative error of at most 0.0053.
Values may be sent and summed in bfloat16 or wider, within the bound.
No kernel may reach another device: no remote copies, remote signals or barrier semaphores. Data moves between devices by JAX's collectives and lax.ppermute only.
A program may use at most 128 MiB of HBM per device.

v0:
```python
import jax
import jax.numpy as jnp
from jax import lax
from jax.sharding import PartitionSpec as P

FFT_LEN = 512
TAPS = 8
CHANNELS = 256


def shifted(value, axis, by):
    length = lax.axis_size(axis)
    pairs = [(i, i + by) for i in range(length) if 0 <= i + by < length]
    return lax.ppermute(value, axis, pairs)


def window_table(taps, length):
    count = taps * length
    position = jnp.arange(count).astype(jnp.float32)
    offset = (position - count / 2 + 0.5) / length
    taper = 0.5 - 0.5 * jnp.cos(2.0 * jnp.pi * (position + 0.5) / count)
    values = jnp.sinc(offset) * taper
    values = values / jnp.sqrt(jnp.sum(values * values))
    return values.reshape(taps, length)


def fourier_table(channels, length):
    channel_index = jnp.arange(channels, dtype=jnp.int32)[:, None]
    sample_index = jnp.arange(length, dtype=jnp.int32)[None, :]
    phase = (channel_index * sample_index % length).astype(jnp.float32) * (2.0 * jnp.pi / length)
    return jnp.stack([jnp.cos(phase), -jnp.sin(phase)], axis=1).astype(jnp.bfloat16)


def per_device(voltages):
    local_inputs = voltages.shape[0]
    slot_spectra = voltages.shape[1] // FFT_LEN
    window = window_table(TAPS, FFT_LEN)
    table = fourier_table(CHANNELS, FFT_LEN)
    tail = voltages[:, (slot_spectra - TAPS + 1) * FFT_LEN :]
    earlier = shifted(tail, ("row", "col"), 1)
    extended = jnp.concatenate([earlier, voltages], axis=1).reshape(
        local_inputs, slot_spectra + TAPS - 1, FFT_LEN
    )
    total = jnp.zeros((local_inputs, slot_spectra, FFT_LEN), jnp.float32)
    for tap_index in range(TAPS):
        total = total + window[tap_index][None, None, :] * extended[
            :, tap_index : tap_index + slot_spectra, :
        ].astype(jnp.float32)
    filtered = total.astype(jnp.bfloat16)
    spectra = jnp.einsum(
        "kpn,isn->kpsi", table, filtered, preferred_element_type=jnp.float32
    ).astype(jnp.bfloat16)
    turned = lax.all_to_all(spectra, "chan", split_axis=0, concat_axis=3, tiled=True)
    inputs_all = turned.shape[3]
    row_count = lax.axis_size("row")
    col_count = lax.axis_size("col")
    row_block = inputs_all // row_count
    col_block = inputs_all // col_count
    spectra_total = slot_spectra * row_count * col_count
    row_start = lax.axis_index("row") * row_block
    col_start = lax.axis_index("col") * col_block
    piece = lax.all_gather(turned, ("row", "col"), axis=2, tiled=True)
    left = lax.dynamic_slice_in_dim(piece, row_start, row_block, 3)
    right = lax.dynamic_slice_in_dim(piece, col_start, col_block, 3)
    flipped = jnp.stack([left[:, 1], -left[:, 0]], axis=1)
    real_part = jnp.einsum("cpsi,cpsj->cij", left, right, preferred_element_type=jnp.float32)
    imag_part = jnp.einsum("cpsi,cpsj->cij", flipped, right, preferred_element_type=jnp.float32)
    summed = jnp.stack([real_part, imag_part], axis=1)
    return summed / spectra_total


def solution(mesh):
    placed = (P("chan", ("row", "col")),)
    return jax.shard_map(
        per_device,
        mesh=mesh,
        in_specs=placed,
        out_specs=P("chan", None, "row", "col"),
        check_vma=False,
    )
```

profile of v0, /device:TPU:1, one launch (start us, length us, event | category | flops | bytes accessed | tf_op | source)
XLA Modules:
  0.0 496.5 jit_solution(200310706514286712)
XLA Ops:
  6.5 1.0 slice.66
  7.5 4.0 collective-permute-start
  11.5 0.7 multiply_reduce_fusion
  12.2 2.2 negate_convert_fusion
  15.0 0.1 broadcast_divide_fusion
  15.1 0.6 collective-permute-done
  15.7 1.7 pad_maximum_fusion
  17.4 2.6 reshape.97
  20.1 11.7 %convert_bitcast_fusion = bf16[256,2,64,32]{0,2,1,3:T(8,128)(2,1)S(1)} fusion(bf16[32,71,512]{2,1,0:T(8,128)(2,1)} %reshape.97, f32[512]{0:T(512)S(1)} %get-tuple-element.8, f32[512]{0:T(512)S(1)} %get-tuple-element.9, f32[512]{0:T(512)S(1)} %get-tuple-element.10, f32[512]{0:T(512)S(1)} %get-tuple-element.11, f32[512]{0:T(512)S(1)} %get-tuple-element.12, ...), kind=kOutput, calls=%fused_computation.16 | convolution fusion | flops 1101004800 | bytes 19415040 | tf_op jit(solution)/shard_map/kpn,isn->kpsi/dot_general | solution.py:50
  31.8 7.6 %copy.12 = bf16[256,2,64,32]{2,1,3,0:T(2,128)(2,1)} copy(bf16[256,2,64,32]{0,2,1,3:T(8,128)(2,1)S(1)} %convert_bitcast_fusion) | data formatting | bytes 4194304 | tf_op jit(solution)/shard_map/convert_element_type | solution.py:52
  39.5 9.1 %reshape.102 = bf16[32,2,16384]{2,1,0:T(2,128)(2,1)S(1)} reshape(bf16[256,32,2,64]{3,2,1,0:T(2,128)(2,1)} %bitcast.26) | data formatting | bytes 4194304
  48.6 62.7 %all_to_all.18 = bf16[32,2,16384]{2,1,0:T(2,128)(2,1)} all-to-all(bf16[32,2,16384]{2,1,0:T(2,128)(2,1)S(1)} %reshape.102), channel_id=1, replica_groups=mesh['chan'=32,'row'=4,'col'=2] {'chan'}, dimensions={0} | all-to-all | bytes 4194304 | tf_op jit(solution)/shard_map/all_to_all | solution.py:53
  111.3 9.8 %reshape.103 = bf16[256,32,2,64]{3,2,1,0:T(2,128)(2,1)} reshape(bf16[32,2,16384]{2,1,0:T(2,128)(2,1)} %all_to_all.18) | data formatting | bytes 4194304
  121.1 3.2 copy.13
  124.3 2.9 copy.14
  127.2 4.8 copy.15
  132.0 0.0 all-gather.2.cloned.1.call-update
  132.0 327.7 %all-gather.2.cloned.1.call-done = bf16[8,2,512,1024]{3,2,1,0:T(8,128)(2,1)} async-done(((bf16[8,2,64,1024]{3,2,1,0:T(8,128)(2,1)}), bf16[8,2,512,1024]{3,2,1,0:T(8,128)(2,1)}) %all-gather.2.cloned.1.call-update) | async-done | bytes 16777232 | tf_op jit(solution)/shard_map/all_gather | solution.py:62
  459.7 4.1 constant_dynamic-slice_fusion
  463.8 9.4 %fusion.8 = f32[8,1,256,512]{3,2,0,1:T(8,128)} fusion(bf16[8,2,512,1024]{3,2,1,0:T(8,128)(2,1)} %all-gather.2.cloned.1.call-done, s32[]{:T(128)S(6)} %select_n.65, s32[]{:T(128)S(6)} %select_n.64), kind=kOutput, calls=%fused_computation.11 | convolution fusion | flops 2147483648 | bytes 16777224 | tf_op jit(solution)/shard_map/cpsi,cpsj->cij/dot_general | solution.py:66
  473.2 1.6 copy-done
  474.7 6.0 %fusion.13 = f32[8,1,256,512]{3,2,0,1:T(8,128)} fusion(bf16[8,2,512,1024]{3,2,1,0:T(8,128)(2,1)S(1)} %copy-done, s32[]{:T(128)S(6)} %select_n.65, bf16[8,1,512,256]{3,2,1,0:T(8,128)(2,1)} %get-tuple-element.6, bf16[8,1,512,256]{3,2,1,0:T(8,128)(2,1)S(1)} %get-tuple-element.5), kind=kOutput, calls=%fused_computation.12 | convolution fusion | flops 2149580800 | bytes 16777220 | tf_op jit(solution)/shard_map/cpsi,cpsj->cij/dot_general | solution.py:67
  480.7 4.5 maximum_multiply_fusion
  485.2 4.4 copy.18
  (3 shorter events, 0.0 us)
Async XLA Ops:
  6.5 453.2 %all-gather.2.cloned.1.call-start = ((), (), s32[]{:S(2)}) async-start(), calls=%async_computation.1 | async-start | bytes 18874368 | tf_op jit(solution)/shard_map/all_gather | solution.py:62
  7.5 8.2 %collective-permute-start = (bf16[32,3584]{1,0:T(8,128)(2,1)S(1)}, bf16[32,3584]{1,0:T(8,128)(2,1)S(1)}, u32[]{:S(2)}, u32[]{:S(2)}) collective-permute-start(bf16[32,3584]{1,0:T(8,128)(2,1)S(1)} %slice.66), channel_id=1, source_target_pairs={{0,1},{1,2},{2,3},{3,4},{4,5},{5,6},{6,7},{8,9},{9,10},{10,11},{11... | collective-permute-start | bytes 688136 | tf_op jit(solution)/shard_map/ppermute | solution.py:14
  463.8 10.9 %copy-start = (bf16[8,2,512,1024]{3,2,1,0:T(8,128)(2,1)S(1)}, bf16[8,2,512,1024]{3,2,1,0:T(8,128)(2,1)}, u32[]{:S(2)}) copy-start(bf16[8,2,512,1024]{3,2,1,0:T(8,128)(2,1)} %all-gather.2.cloned.1.call-done) | copy-start | bytes 50331652
Sparse Core Ops, SparseCore 0:
  132.1 327.5 all-gather.1
where the time goes:
time: 497 us
  waiting for transfers between devices  328 us (66%)
  blocking collectives  62.7 us (13%)
  local copies, waits for them, and re-layouts  47.1 us (9%)
  matrix products  27.1 us (5%)
  between operations  14.2 us (3%)
  other arithmetic  13.3 us (3%)
    all_gather x1, waiting for transfers between devices, per_device(): piece = lax.all_gather(turned, ('row', 'col'), axis=2, tiled=True)  328 us
    all_to_all x1, blocking collectives, per_device(): lax.all_to_all(spectra, 'chan', split_axis=0, concat_axis=3, tiled=True)  62.7 us
    unnamed x4, local copies, waits for them, and re-layouts  20.5 us
    dot_general x1, matrix products, per_device(): jnp.einsum('kpn,isn->kpsi', table, filtered, preferred_element_type=jnp.f...  11.7 us
    all_to_all x3, local copies, waits for them, and re-layouts, per_device(): lax.all_to_all(spectra, 'chan', split_axis=0, concat_axis=3, tiled=True)  10.9 us
  transfers between devices with their start and end apart: 2, of which 2 were waited for; matrix products, arithmetic and copies ran while one was open for 1% of the time, Pallas kernels for 0%

commit v1 on v0

v1 whole, which is shorter than its diff:
```python
import functools

import jax
import jax.numpy as jnp
import ml_dtypes
import numpy as np
from jax import lax
from jax.experimental import pallas as pl
from jax.experimental.pallas import tpu as pltpu
from jax.sharding import PartitionSpec as P

FFT_LEN = 512
TAPS = 8
CHANNELS = 256
LANES = 128


def window_table(taps, length):
    count = taps * length
    position = np.arange(count, dtype=np.float64)
    offset = (position - count / 2 + 0.5) / length
    taper = 0.5 - 0.5 * np.cos(2.0 * np.pi * (position + 0.5) / count)
    values = np.sinc(offset) * taper
    values = values / np.sqrt(np.sum(values * values))
    return values.reshape(taps, length).astype(np.float32)


def fourier_table(channels, length):
    channel_index = np.arange(channels)[:, None]
    sample_index = np.arange(length)[None, :]
    phase = (channel_index * sample_index % length) * (2.0 * np.pi / length)
    return np.stack([np.cos(phase), -np.sin(phase)]).astype(np.float32).astype(ml_dtypes.bfloat16)


def channelize_kernel(v_ref, h_ref, w_ref, tab_ref, o_ref, f_ref, t_ref):
    inputs = v_ref.shape[0]
    spectra = v_ref.shape[1] // FFT_LEN
    row_tile = 16
    n_chunks = FFT_LEN // LANES

    def fir(step, carry):
        first_row = pl.multiple_of((step // n_chunks) * row_tile, row_tile)
        chunk = step % n_chunks
        lane = pl.multiple_of(chunk * LANES, LANES)
        rows = pl.ds(first_row, row_tile)
        taps = [w_ref[t : t + 1, pl.ds(lane, LANES)] for t in range(TAPS)]
        taps = [jnp.broadcast_to(t, (row_tile, LANES)) for t in taps]
        sums = {}
        for block in range(spectra + TAPS - 1):
            if block < TAPS - 1:
                value = h_ref[rows, pl.ds(block * FFT_LEN + lane, LANES)]
            else:
                value = v_ref[rows, pl.ds((block - TAPS + 1) * FFT_LEN + lane, LANES)]
            value = value.astype(jnp.float32)
            for t in range(TAPS):
                s = block - t
                if 0 <= s < spectra:
                    term = taps[t] * value
                    sums[s] = term if t == 0 else sums[s] + term
            done = block - TAPS + 1
            if done >= 0:
                f_ref[chunk, pl.ds(first_row * spectra + done, row_tile, stride=spectra), :] = sums.pop(done)
        return carry

    lax.fori_loop(0, (inputs // row_tile) * n_chunks, fir, 0)

    group = 8
    low = lax.broadcasted_iota(jnp.int32, (CHANNELS, LANES), 1) < spectra

    def dft(step, carry):
        start = pl.multiple_of(step * group * spectra, group * spectra)
        rows = pl.ds(start, group * spectra)
        block = jnp.concatenate([f_ref[c, rows, :].astype(jnp.bfloat16) for c in range(n_chunks)], axis=1)
        dims = (((1,), (1,)), ((), ()))
        real = lax.dot_general(tab_ref[0], block, dims, preferred_element_type=jnp.float32)
        imag = lax.dot_general(tab_ref[1], block, dims, preferred_element_type=jnp.float32)
        for pair in range(group // 2):
            cut = slice(pair * LANES, (pair + 1) * LANES)
            re, im = real[:, cut], imag[:, cut]
            even = jnp.where(low, re, pltpu.roll(im, spectra, 1))
            odd = jnp.where(low, pltpu.roll(re, spectra, 1), im)
            row = step * group + 2 * pair
            t_ref[pl.ds(row, CHANNELS, stride=inputs), :] = even
            t_ref[pl.ds(row + 1, CHANNELS, stride=inputs), :] = odd
        return carry

    lax.fori_loop(0, inputs // group, dft, 0)

    chunk = 16

    def cast(step, carry):
        first = pl.multiple_of(step * chunk, chunk)
        rows = t_ref[pl.ds(first * inputs, chunk * inputs), :]
        o_ref[pl.ds(first, chunk)] = rows.astype(jnp.bfloat16).reshape(chunk, inputs, LANES)
        return carry

    lax.fori_loop(0, CHANNELS // chunk, cast, 0)


def channelize(voltages, earlier):
    inputs = voltages.shape[0]
    spectra = voltages.shape[1] // FFT_LEN
    vmem = pl.BlockSpec(memory_space=pltpu.VMEM)
    return pl.pallas_call(
        channelize_kernel,
        out_shape=jax.ShapeDtypeStruct((CHANNELS, inputs, 2 * spectra), jnp.bfloat16),
        in_specs=[vmem] * 4,
        out_specs=vmem,
        scratch_shapes=[
            pltpu.VMEM((FFT_LEN // LANES, inputs * spectra, LANES), jnp.float32),
            pltpu.VMEM((CHANNELS * inputs, 2 * spectra), jnp.float32),
        ],
        compiler_params=pltpu.CompilerParams(vmem_limit_bytes=32 << 20),
        name="channelize",
    )(voltages, earlier, window_table(TAPS, FFT_LEN), fourier_table(CHANNELS, FFT_LEN))


def correlate_kernel(groups, slots, scale, r_ref, o_ref, x_ref, y_ref):
    height = r_ref.shape[1]

    @pl.when(pl.program_id(0) == 0)
    def _():
        half = LANES // 2
        upper = lax.broadcasted_iota(jnp.int32, (height, LANES), 1) >= half

        def place(g, carry):
            rows = pl.ds(pl.multiple_of(g * height, height), height)
            for t in range(slots):
                lanes = slice(t * LANES, (t + 1) * LANES)
                value = r_ref[g * slots + t]
                turned = pltpu.roll(value.astype(jnp.float32), half, 1)
                x_ref[rows, lanes] = value
                y_ref[rows, lanes] = jnp.where(upper, -turned, turned).astype(jnp.bfloat16)
            return carry

        lax.fori_loop(0, groups, place, 0)

    row_block, col_block = o_ref.shape[2], o_ref.shape[3]
    col_count = x_ref.shape[0] // col_block
    row = pl.multiple_of((pl.program_id(0) // col_count) * row_block, row_block)
    col = pl.multiple_of((pl.program_id(0) % col_count) * col_block, col_block)
    right = x_ref[pl.ds(col, col_block), :]
    dims = (((1,), (1,)), ((), ()))
    for part, ref in enumerate((x_ref, y_ref)):
        left = ref[pl.ds(row, row_block), :]
        value = lax.dot_general(left, right, dims, preferred_element_type=jnp.float32)
        o_ref[0, part] = (value * scale).astype(jnp.bfloat16)


def correlate(received, groups, slots, row_count, col_count, scale):
    height = received.shape[1]
    total = groups * height
    row_block, col_block = total // row_count, total // col_count
    tiles = row_count * col_count
    return pl.pallas_call(
        functools.partial(correlate_kernel, groups, slots, scale),
        grid=(tiles,),
        out_shape=jax.ShapeDtypeStruct((tiles, 2, row_block, col_block), jnp.bfloat16),
        in_specs=[pl.BlockSpec(memory_space=pltpu.VMEM)],
        out_specs=pl.BlockSpec((1, 2, row_block, col_block), lambda i: (i, 0, 0, 0)),
        scratch_shapes=[pltpu.VMEM((total, slots * LANES), jnp.bfloat16)] * 2,
        compiler_params=pltpu.CompilerParams(vmem_limit_bytes=32 << 20),
        name="correlate",
    )(received)


def per_device(voltages):
    slot_spectra = voltages.shape[1] // FFT_LEN
    row_count = lax.axis_size("row")
    col_count = lax.axis_size("col")
    slots = row_count * col_count
    groups = lax.axis_size("chan")
    tail = voltages[:, (slot_spectra - TAPS + 1) * FFT_LEN :]
    earlier = lax.ppermute(tail, ("row", "col"), [(i, i + 1) for i in range(slots - 1)])
    spectra = channelize(voltages, earlier)
    turned = lax.all_to_all(spectra, ("chan", "row", "col"), split_axis=0, concat_axis=0, tiled=True)
    tiles = correlate(turned, groups, slots, row_count, col_count, 1.0 / (slot_spectra * slots))
    summed = lax.all_to_all(tiles, ("row", "col"), split_axis=0, concat_axis=0, tiled=True)
    return summed.astype(jnp.float32)


def solution(mesh):
    placed = (P("chan", ("row", "col")),)
    return jax.shard_map(
        per_device,
        mesh=mesh,
        in_specs=placed,
        out_specs=P("chan", None, "row", "col"),
        check_vma=False,
    )
```

time: 497 us -> 159 us (0.32)
  waiting for transfers between devices: 328 us -> 4.24 us
  blocking collectives: 62.7 us -> 124 us
  local copies, waits for them, and re-layouts: 47.1 us -> 4.3 us
  matrix products: 27.1 us -> 0 us
  Pallas kernels: 0 us -> 17.7 us
  between operations: 14.2 us -> 0.03 us
  other arithmetic: 13.3 us -> 4.55 us
    all_gather x1 -> x0, waiting for transfers between devices: 328 us -> none  [per_device(): piece = lax.all_gather(turned, ('row', 'col'), axis=2, tiled=True)]
    all_to_all x1 -> x2, blocking collectives: 62.7 us -> 124 us  [the longest x1 72.4 us: per_device(): lax.all_to_all(spectra, ('chan', 'row', 'col'), split_axis=0, concat_axis...]
    dot_general x3 -> x0, matrix products: 27.1 us -> none  [the longest x1 11.7 us: per_device(): jnp.einsum('kpn,isn->kpsi', table, filtered, preferred_element_type=jnp.f...]
    pallas_call x0 -> x2, Pallas kernels: none -> 17.7 us  [the longest x1 8.96 us: correlate(): pl.pallas_call(functools.partial(correlate_kernel, groups, slots, scale),...]
    unnamed x4 -> x6, local copies, waits for them, and re-layouts: 20.5 us -> 3.35 us
    all_to_all x3 -> x0, local copies, waits for them, and re-layouts: 10.9 us -> none  [per_device(): lax.all_to_all(spectra, 'chan', split_axis=0, concat_axis=3, tiled=True)]
    convert_element_type x1 -> x0, local copies, waits for them, and re-layouts: 7.64 us -> none  [per_device(): spectra = jnp.einsum('kpn,isn->kpsi', table, filtered, preferred_element_...]
  transfers between devices with their start and end apart: 2 -> 1, of which waited for: 2 -> 1; matrix products, arithmetic and copies ran while one was open for 1% -> 0% of each run, Pallas kernels for 0% -> 0%
where the time goes in v1:
time: 159 us
  blocking collectives  124 us (78%)
  Pallas kernels  17.7 us (11%)
  other arithmetic  4.55 us (3%)
  local copies, waits for them, and re-layouts  4.3 us (3%)
  waiting for transfers between devices  4.24 us (3%)
  starting transfers between devices  3.96 us (2%)
    all_to_all x1, blocking collectives, per_device(): lax.all_to_all(spectra, ('chan', 'row', 'col'), split_axis=0, concat_axis...  72.4 us
    all_to_all x1, blocking collectives, per_device(): lax.all_to_all(tiles, ('row', 'col'), split_axis=0, concat_axis=0, tiled=...  51.6 us
    pallas_call x1, Pallas kernels, correlate(): pl.pallas_call(functools.partial(correlate_kernel, groups, slots, scale),...  8.96 us
    pallas_call x1, Pallas kernels, channelize(): pl.pallas_call(channelize_kernel, out_shape=jax.ShapeDtypeStruct((CHANNEL...  8.73 us
    convert_element_type x1, other arithmetic, per_device(): return summed.astype(jnp.float32)  4.55 us
    ppermute x1, waiting for transfers between devices, per_device(): lax.ppermute(tail, ('row', 'col'), [(i, i + 1) for i in range(slots - 1)])  4.24 us
    ppermute x1, starting transfers between devices, per_device(): lax.ppermute(tail, ('row', 'col'), [(i, i + 1) for i in range(slots - 1)])  3.96 us
    unnamed x6, local copies, waits for them, and re-layouts  3.35 us
  transfers between devices with their start and end apart: 1, of which 1 were waited for; matrix products, arithmetic and copies ran while one was open for 0% of the time, Pallas kernels for 0%

profile of v1, /device:TPU:1, one launch (start us, length us, event | category | flops | bytes accessed | tf_op | source)
XLA Modules:
  0.0 158.8 jit_solution(14510660454722746095)
XLA Ops:
  0.0 1.0 slice.3
  1.0 4.0 %collective-permute-start = (bf16[32,3584]{1,0:T(8,128)(2,1)S(1)}, bf16[32,3584]{1,0:T(8,128)(2,1)S(1)}, u32[]{:S(2)}, u32[]{:S(2)}) collective-permute-start(bf16[32,3584]{1,0:T(8,128)(2,1)S(1)} %slice.3), channel_id=1, source_target_pairs={{0,1},{1,2},{2,3},{3,4},{4,5},{5,6},{6,7},{8,9},{9,10},{10,11},{11... | collective-permute-start | bytes 688136 | tf_op jit(solution)/shard_map/ppermute | solution.py:174
  4.9 4.2 %collective-permute-done.h_ref = bf16[32,3584]{1,0:T(8,128)(2,1)S(1)} collective-permute-done((bf16[32,3584]{1,0:T(8,128)(2,1)S(1)}, bf16[32,3584]{1,0:T(8,128)(2,1)S(1)}, u32[]{:S(2)}, u32[]{:S(2)}) %collective-permute-start) | collective-permute-done | bytes 229408 | tf_op jit(solution)/shard_map/ppermute | solution.py:174
  9.2 0.0 copy-start
  9.2 1.6 %copy-done = bf16[32,32768]{1,0:T(8,128)(2,1)S(1)} copy-done((bf16[32,32768]{1,0:T(8,128)(2,1)S(1)}, bf16[32,32768]{1,0:T(8,128)(2,1)}, u32[]{:S(2)}) %copy-start) | copy-done | bytes 2097176
  10.8 0.0 copy-start.1
  10.8 1.0 copy-done.1
  11.8 0.0 copy-start.2
  11.8 0.7 copy-done.2
  12.5 8.7 %channelize.1 = bf16[256,32,128]{2,1,0:T(8,128)(2,1)S(1)} custom-call(bf16[32,32768]{1,0:T(8,128)(2,1)S(1)} %copy-done, bf16[32,3584]{1,0:T(8,128)(2,1)S(1)} %collective-permute-done.h_ref, f32[8,512]{1,0:T(8,128)S(1)} %copy-done.2, bf16[2,256,512]{2,1,0:T(8,128)(2,1)S(1)} %copy-done.1), custom_call_target="tpu_custom_call" | custom-call | tf_op jit(solution)/shard_map/channelize/pallas_call | solution.py:104
  21.3 72.4 %all_to_all.10.r_ref = bf16[256,32,128]{2,1,0:T(8,128)(2,1)S(1)} all-to-all(bf16[256,32,128]{2,1,0:T(8,128)(2,1)S(1)} %channelize.1), channel_id=1, replica_groups=mesh['chan'=32,'row'=4,'col'=2] {'chan','row','col'}, dimensions={0} | all-to-all | bytes 4194304 | tf_op jit(solution)/shard_map/all_to_all | solution.py:176
  93.6 9.0 %correlate.1 = bf16[8,2,256,512]{3,2,1,0:T(8,128)(2,1)S(1)} custom-call(bf16[256,32,128]{2,1,0:T(8,128)(2,1)S(1)} %all_to_all.10.r_ref), custom_call_target="tpu_custom_call" | custom-call | tf_op jit(solution)/shard_map/correlate/pallas_call | solution.py:155
  102.6 51.6 %all_to_all.11 = bf16[8,2,256,512]{3,2,1,0:T(8,128)(2,1)S(1)} all-to-all(bf16[8,2,256,512]{3,2,1,0:T(8,128)(2,1)S(1)} %correlate.1), channel_id=1, replica_groups=mesh['chan'=32,'row'=4,'col'=2] {'row','col'}, dimensions={0} | all-to-all | bytes 8388608 | tf_op jit(solution)/shard_map/all_to_all | solution.py:178
  154.2 4.5 %convert_element_type.3 = f32[8,2,256,512]{3,2,1,0:T(8,128)} convert(bf16[8,2,256,512]{3,2,1,0:T(8,128)(2,1)S(1)} %all_to_all.11) | non-fusion elementwise | flops 2097152 | bytes 12582912 | tf_op jit(solution)/shard_map/convert_element_type | solution.py:179
Async XLA Ops:
  1.0 8.2 %collective-permute-start = (bf16[32,3584]{1,0:T(8,128)(2,1)S(1)}, bf16[32,3584]{1,0:T(8,128)(2,1)S(1)}, u32[]{:S(2)}, u32[]{:S(2)}) collective-permute-start(bf16[32,3584]{1,0:T(8,128)(2,1)S(1)} %slice.3), channel_id=1, source_target_pairs={{0,1},{1,2},{2,3},{3,4},{4,5},{5,6},{6,7},{8,9},{9,10},{10,11},{11... | collective-permute-start | bytes 688136 | tf_op jit(solution)/shard_map/ppermute | solution.py:174
  9.2 1.6 %copy-start = (bf16[32,32768]{1,0:T(8,128)(2,1)S(1)}, bf16[32,32768]{1,0:T(8,128)(2,1)}, u32[]{:S(2)}) copy-start(bf16[32,32768]{1,0:T(8,128)(2,1)} %v_ref.1) | copy-start | bytes 6291460
  10.8 1.0 copy-start.1
  11.8 0.7 copy-start.2

commit v2 on v0

v2 whole, which is shorter than its diff:
```python
import functools

import jax
import jax.numpy as jnp
import ml_dtypes
import numpy as np
from jax import lax
from jax.experimental import pallas as pl
from jax.experimental.pallas import tpu as pltpu
from jax.sharding import PartitionSpec as P

FFT_LEN = 512
TAPS = 8
CHANNELS = 256
LANES = 128
CORES = 2
HEAD = 8
CHUNKS = FFT_LEN // LANES
ALL = ("chan", "row", "col")
VMEM = pl.BlockSpec(memory_space=pltpu.VMEM)
SMEM = pl.BlockSpec(memory_space=pltpu.SMEM)
NT = (((1,), (1,)), ((), ()))


def window_table(taps, length):
    count = taps * length
    position = np.arange(count, dtype=np.float64)
    offset = (position - count / 2 + 0.5) / length
    taper = 0.5 - 0.5 * np.cos(2.0 * np.pi * (position + 0.5) / count)
    values = np.sinc(offset) * taper
    values = values / np.sqrt(np.sum(values * values))
    return values.reshape(taps, length).astype(np.float32)


def fourier_table(channels, length):
    channel_index = np.arange(channels)[:, None]
    sample_index = np.arange(length)[None, :]
    phase = (channel_index * sample_index % length) * (2.0 * np.pi / length)
    return np.stack([np.cos(phase), -np.sin(phase)]).astype(np.float32).astype(ml_dtypes.bfloat16)


def chunk_channels(chunk, rows, cols):
    slots = rows * cols
    pairs = CHANNELS // (CORES * slots)
    found = []
    for pair in range(pairs):
        for row in range(rows):
            for col in range(cols):
                core = col if chunk == 0 else 1 - col
                found.append((pair * CORES + core) * slots + row * cols + col)
    return np.array(found)


def fir_rows(read, first, last, store, w_ref, rows, lane):
    height = rows.size
    taps = [jnp.broadcast_to(w_ref[t : t + 1, pl.ds(lane, LANES)], (height, LANES)) for t in range(TAPS)]
    sums = {}
    for block in range(first, last + TAPS - 1):
        value = read(block).astype(jnp.float32)
        for t in range(TAPS):
            s = block - t
            if first <= s < last:
                term = taps[t] * value
                sums[s] = term if t == 0 else sums[s] + term
        done = block - TAPS + 1
        if done >= first:
            store(done, sums.pop(done))


def for_tiles(inputs, body):
    row_tile = 16

    def step(index, carry):
        chunk = index % CHUNKS
        first_row = pl.multiple_of((index // CHUNKS) * row_tile, row_tile)
        body(pl.ds(first_row, row_tile), first_row, chunk, pl.multiple_of(chunk * LANES, LANES))
        return carry

    lax.fori_loop(0, (inputs // row_tile) * CHUNKS, step, 0)


def fir_kernel(v_ref, w_ref, f_ref):
    inputs = v_ref.shape[0]
    spectra = v_ref.shape[1] // FFT_LEN
    body_len = spectra - HEAD

    def tile(rows, first_row, chunk, lane):
        def read(block):
            return v_ref[rows, pl.ds((block - TAPS + 1) * FFT_LEN + lane, LANES)]

        def store(s, value):
            f_ref[chunk, pl.ds(first_row * body_len + s - HEAD, rows.size, stride=body_len), :] = value

        fir_rows(read, HEAD, spectra, store, w_ref, rows, lane)

    for_tiles(inputs, tile)


def dft(f_ref, head_ref, tab_ref, o_ref, t_ref):
    inputs = o_ref.shape[1] * CORES
    channels = tab_ref.shape[0] // 2
    body_len = f_ref.shape[1] // inputs
    spectra = body_len + HEAD
    group = 8
    low = lax.broadcasted_iota(jnp.int32, (channels, LANES), 1) < spectra

    def transform(step, carry):
        columns = []
        for c in range(CHUNKS):
            parts = []
            for j in range(group):
                i = step * group + j
                parts.append(head_ref[c, pl.ds(pl.multiple_of(i * HEAD, HEAD), HEAD), :])
                parts.append(f_ref[c, pl.ds(pl.multiple_of(i * body_len, 8), body_len), :])
            columns.append(jnp.concatenate(parts, axis=0).astype(jnp.bfloat16))
        block = jnp.concatenate(columns, axis=1)
        both = lax.dot_general(tab_ref[...], block, NT, preferred_element_type=jnp.float32)
        for pair in range(group // 2):
            cut = slice(pair * LANES, (pair + 1) * LANES)
            re, im = both[:channels, cut], both[channels:, cut]
            even = jnp.where(low, re, pltpu.roll(im, spectra, 1))
            odd = jnp.where(low, pltpu.roll(re, spectra, 1), im)
            row = step * group + 2 * pair
            t_ref[pl.ds(row, channels, stride=inputs), :] = even
            t_ref[pl.ds(row + 1, channels, stride=inputs), :] = odd
        return carry

    lax.fori_loop(0, inputs // group, transform, 0)

    half = inputs // CORES
    slots = 8

    def cast(pair, carry):
        for core in range(CORES):
            for slot in range(slots):
                first = pl.multiple_of((pair * slots + slot) * inputs + core * half, half)
                rows = t_ref[pl.ds(first, half), :]
                o_ref[pair * (CORES * slots) + core * slots + slot] = rows.astype(jnp.bfloat16)
        return carry

    lax.fori_loop(0, channels // slots, cast, 0)


def head_kernel(v_ref, h_ref, f_ref, w_ref, tab_ref, o_ref, head_ref, t_ref):
    def tile(rows, first_row, chunk, lane):
        def read(block):
            if block < TAPS - 1:
                return h_ref[rows, pl.ds(block * FFT_LEN + lane, LANES)]
            return v_ref[rows, pl.ds((block - TAPS + 1) * FFT_LEN + lane, LANES)]

        def store(s, value):
            head_ref[chunk, pl.ds(first_row * HEAD + s, rows.size, stride=HEAD), :] = value

        fir_rows(read, 0, HEAD, store, w_ref, rows, lane)

    for_tiles(v_ref.shape[0], tile)
    dft(f_ref, head_ref, tab_ref, o_ref, t_ref)


def params(mib=24):
    return pltpu.CompilerParams(vmem_limit_bytes=mib << 20)


def cost(flops, nbytes):
    return pl.CostEstimate(flops=flops, bytes_accessed=nbytes, transcendentals=0)


def channelize(voltages, earlier, rows, cols):
    inputs = voltages.shape[0]
    spectra = voltages.shape[1] // FFT_LEN
    window = window_table(TAPS, FFT_LEN)
    table = fourier_table(CHANNELS, FFT_LEN)
    tables = [table[:, chunk_channels(c, rows, cols)].reshape(-1, FFT_LEN) for c in range(2)]
    channels = CHANNELS // 2
    body = pl.pallas_call(
        fir_kernel,
        out_shape=jax.ShapeDtypeStruct((CHUNKS, inputs * (spectra - HEAD), LANES), jnp.float32),
        in_specs=[VMEM] * 2,
        out_specs=VMEM,
        compiler_params=params(),
        cost_estimate=cost(16 * voltages.size, 6 * voltages.size),
        name="fir",
    )(voltages, window)
    message = jax.ShapeDtypeStruct((CHANNELS, inputs // CORES, 2 * spectra), jnp.bfloat16)
    scratch = [pltpu.VMEM((channels * inputs, 2 * spectra), jnp.float32)]
    work = cost(4 * channels * FFT_LEN * inputs * spectra, 6 * voltages.size)
    first, head = pl.pallas_call(
        head_kernel,
        out_shape=[message, jax.ShapeDtypeStruct((CHUNKS, inputs * HEAD, LANES), jnp.float32)],
        in_specs=[VMEM] * 5,
        out_specs=[VMEM] * 2,
        scratch_shapes=scratch,
        compiler_params=params(),
        cost_estimate=work,
        name="head_dft",
    )(voltages[:, : HEAD * FFT_LEN], earlier, body, window, tables[0])
    second = pl.pallas_call(
        dft,
        out_shape=message,
        in_specs=[VMEM] * 3,
        out_specs=VMEM,
        scratch_shapes=scratch,
        compiler_params=params(),
        cost_estimate=work,
        name="dft",
    )(body, head, tables[1])
    return first, second


def correlate_kernel(groups, rows, cols, scale, at_ref, mine_ref, other_ref, *refs):
    outs, (x_ref, y_ref) = refs[:-2], refs[-2:]
    core, row = at_ref[0], at_ref[1]
    part = mine_ref.shape[1]
    height = CORES * part
    slots = rows * cols
    half = LANES // 2

    def place(g, carry):
        for ref, owner in ((mine_ref, core), (other_ref, 1 - core)):
            dest = pl.ds(pl.multiple_of(g * height + owner * part, part), part)
            for t in range(slots):
                x_ref[dest, t * LANES : (t + 1) * LANES] = ref[g * slots + t]
        return carry

    lax.fori_loop(0, groups, place, 0)

    row_block = groups * height // rows
    row_half = row_block // CORES
    col_block = groups * height // cols
    upper = lax.broadcasted_iota(jnp.int32, (row_half, LANES), 1) >= half
    for dy in range(rows):
        first = pl.multiple_of(lax.rem(row + dy, rows) * row_block + core * row_half, row_half)
        left = pl.ds(first, row_half)
        for t in range(slots):
            lanes = slice(t * LANES, (t + 1) * LANES)
            turned = pltpu.roll(x_ref[left, lanes].astype(jnp.float32), half, 1)
            y_ref[:, lanes] = jnp.where(upper, -turned, turned).astype(jnp.bfloat16)
        for d in range(cols):
            col = jnp.bitwise_xor(core, d)
            right = x_ref[pl.ds(pl.multiple_of(col * col_block, col_block), col_block), :]
            real = lax.dot_general(x_ref[left, :], right, NT, preferred_element_type=jnp.float32)
            imag = lax.dot_general(y_ref[...], right, NT, preferred_element_type=jnp.float32)
            out = outs[dy * cols + d]
            out[0] = (real * scale).astype(jnp.bfloat16)
            out[1] = (imag * scale).astype(jnp.bfloat16)


def correlate(at, mine, other, groups, rows, cols, scale):
    total = groups * mine.shape[1] * CORES
    depth = rows * cols * LANES
    row_half, col_block = total // rows // CORES, total // cols
    piece = jax.ShapeDtypeStruct((2, row_half, col_block), jnp.bfloat16)
    return pl.pallas_call(
        functools.partial(correlate_kernel, groups, rows, cols, scale),
        out_shape=[piece] * (rows * cols),
        in_specs=[SMEM, VMEM, VMEM],
        out_specs=[VMEM] * (rows * cols),
        scratch_shapes=[pltpu.VMEM((total, depth), jnp.bfloat16), pltpu.VMEM((row_half, depth), jnp.bfloat16)],
        compiler_params=params(),
        cost_estimate=cost(2 * total * total * depth, 8 * total * depth),
        name="correlate",
    )(at, mine, other)


def widen_kernel(count, aliased, where_ref, *refs):
    o_ref = refs[-1]
    for j in range(count):

        @pl.when(pl.program_id(0) == j)
        def _():
            o_ref[0] = refs[aliased + j][...].astype(jnp.float32)


def widen(pieces, where, shape, into=None):
    _, row_half, col_block = pieces[0].shape
    aliased = 0 if into is None else 1
    spec = pltpu.PrefetchScalarGridSpec(
        num_scalar_prefetch=1,
        grid=(len(pieces),),
        in_specs=[pl.BlockSpec(memory_space=pl.ANY)] * aliased + [VMEM] * len(pieces),
        out_specs=pl.BlockSpec((1, 2, row_half, col_block), lambda j, at: (at[0, j], 0, at[1, j], 0)),
    )
    return pl.pallas_call(
        functools.partial(widen_kernel, len(pieces), aliased),
        grid_spec=spec,
        out_shape=jax.ShapeDtypeStruct(shape, jnp.float32),
        input_output_aliases={1: 0} if aliased else {},
        compiler_params=params(),
        cost_estimate=cost(len(pieces) * pieces[0].size, 6 * len(pieces) * pieces[0].size),
        name="widen",
    )(where, *([] if into is None else [into]), *pieces)


def per_device(voltages):
    slot_spectra = voltages.shape[1] // FFT_LEN
    rows = lax.axis_size("row")
    cols = lax.axis_size("col")
    slots = rows * cols
    groups = lax.axis_size("chan")
    tail = voltages[:, (slot_spectra - TAPS + 1) * FFT_LEN :]
    earlier = lax.ppermute(tail, ("row", "col"), [(i, i + 1) for i in range(slots - 1)])
    core = lax.axis_index("chan") % CORES
    row, col = lax.axis_index("row"), lax.axis_index("col")
    at = jnp.stack([core, row]).astype(jnp.int32)
    scale = 1.0 / (slot_spectra * slots)
    total = groups * voltages.shape[0]
    shape = (slots, 2, total // rows, total // cols)
    messages = channelize(voltages, earlier, rows, cols)
    swap = [(i, i ^ 1) for i in range(groups)]
    arrived = [lax.all_to_all(message, ALL, split_axis=0, concat_axis=0, tiled=True) for message in messages]
    out = None
    for chunk, mine in enumerate(arrived):
        if chunk:
            mine, got = lax.optimization_barrier((mine, got))
            out = widen(got, where, shape)
        other = lax.ppermute(mine, "chan", swap)
        sent = correlate(at, mine, other, groups, rows, cols, scale)
        got, channel, half = [], [], []
        for dy in range(rows):
            for d in range(cols):
                pairs = []
                for c in range(groups):
                    for r in range(rows):
                        for x in range(cols):
                            to_core = x if chunk == 0 else 1 - x
                            target = (c - c % CORES + to_core, (r + dy) % rows, (c % CORES) ^ d)
                            pairs.append(((c * rows + r) * cols + x, (target[0] * rows + target[1]) * cols + target[2]))
                got.append(lax.ppermute(sent[dy * cols + d], ALL, pairs))
                from_col = core if chunk == 0 else 1 - core
                channel.append((row + rows - dy) % rows * cols + from_col)
                half.append(jnp.bitwise_xor(col, d))
        where = jnp.stack([jnp.stack(channel), jnp.stack(half)]).astype(jnp.int32)
    return widen(got, where, shape, out)


def solution(mesh):
    placed = (P("chan", ("row", "col")),)
    return jax.shard_map(
        per_device,
        mesh=mesh,
        in_specs=placed,
        out_specs=P("chan", None, "row", "col"),
        check_vma=False,
    )
```

time: 497 us -> 170 us (0.34)
  waiting for transfers between devices: 328 us -> 60 us
  blocking collectives: 62.7 us -> 0 us
  starting transfers between devices: 3.96 us -> 63.5 us
  local copies, waits for them, and re-layouts: 47.1 us -> 12.2 us
  Pallas kernels: 0 us -> 33.8 us
  matrix products: 27.1 us -> 0 us
  between operations: 14.2 us -> 0.17 us
  other arithmetic: 13.3 us -> 0.09 us
    all_gather x1 -> x0, waiting for transfers between devices: 328 us -> none  [per_device(): piece = lax.all_gather(turned, ('row', 'col'), axis=2, tiled=True)]
    all_to_all x1 -> x0, blocking collectives: 62.7 us -> none  [per_device(): lax.all_to_all(spectra, 'chan', split_axis=0, concat_axis=3, tiled=True)]
    ppermute x1 -> x19, starting transfers between devices: 3.96 us -> 41.9 us  [the longest x16 31 us: per_device(): got.append(lax.ppermute(sent[dy * cols + d], ALL, pairs))]
    pallas_call x0 -> x7, Pallas kernels: none -> 33.8 us  [the longest x2 14.8 us: correlate(): pl.pallas_call(functools.partial(correlate_kernel, groups, rows, cols, sc...]
    ppermute x1 -> x19, waiting for transfers between devices: 0.56 us -> 33.5 us  [the longest x16 29 us: per_device(): got.append(lax.ppermute(sent[dy * cols + d], ALL, pairs))]
    dot_general x3 -> x0, matrix products: 27.1 us -> none  [the longest x1 11.7 us: per_device(): jnp.einsum('kpn,isn->kpsi', table, filtered, preferred_element_type=jnp.f...]
    all_to_all x0 -> x2, waiting for transfers between devices: none -> 26.5 us  [per_device(): lax.all_to_all(message, ALL, split_axis=0, concat_axis=0, tiled=True)]
    all_to_all x0 -> x2, starting transfers between devices: none -> 21.7 us  [per_device(): lax.all_to_all(message, ALL, split_axis=0, concat_axis=0, tiled=True)]
  transfers between devices with their start and end apart: 2 -> 21, of which waited for: 2 -> 9; matrix products, arithmetic and copies ran while one was open for 1% -> 1% of each run, Pallas kernels for 0% -> 10%
where the time goes in v2:
time: 170 us
  starting transfers between devices  63.5 us (37%)
  waiting for transfers between devices  60 us (35%)
  Pallas kernels  33.8 us (20%)
  local copies, waits for them, and re-layouts  12.2 us (7%)
    ppermute x16, starting transfers between devices, per_device(): got.append(lax.ppermute(sent[dy * cols + d], ALL, pairs))  31 us
    ppermute x16, waiting for transfers between devices, per_device(): got.append(lax.ppermute(sent[dy * cols + d], ALL, pairs))  29 us
    all_to_all x2, waiting for transfers between devices, per_device(): lax.all_to_all(message, ALL, split_axis=0, concat_axis=0, tiled=True)  26.5 us
    all_to_all x2, starting transfers between devices, per_device(): lax.all_to_all(message, ALL, split_axis=0, concat_axis=0, tiled=True)  21.7 us
    pallas_call x2, Pallas kernels, correlate(): pl.pallas_call(functools.partial(correlate_kernel, groups, rows, cols, sc...  14.8 us
    unnamed x24, local copies, waits for them, and re-layouts  9.98 us
    pallas_call x2, Pallas kernels, widen(): pl.pallas_call(functools.partial(widen_kernel, len(pieces), aliased), gri...  8.34 us
    ppermute x2, starting transfers between devices, per_device(): other = lax.ppermute(mine, 'chan', swap)  6.95 us
  transfers between devices with their start and end apart: 21, of which 9 were waited for; matrix products, arithmetic and copies ran while one was open for 1% of the time, Pallas kernels for 10%

profile of v2, /device:TPU:1, one launch (start us, length us, event | category | flops | bytes accessed | tf_op | source)
XLA Modules:
  0.0 169.8 jit_solution(14367680021457710422)
XLA Ops:
  1.0 4.0 %collective-permute-start = (bf16[32,3584]{1,0:T(8,128)(2,1)S(1)}, bf16[32,3584]{1,0:T(8,128)(2,1)S(1)}, u32[]{:S(2)}, u32[]{:S(2)}) collective-permute-start(bf16[32,3584]{1,0:T(8,128)(2,1)S(1)} %slice.7), channel_id=1, source_target_pairs={{0,1},{1,2},{2,3},{3,4},{4,5},{5,6},{6,7},{8,9},{9,10},{10,11},{11... | collective-permute-start | bytes 688136 | tf_op jit(solution)/shard_map/ppermute | solution.py:301
  11.2 4.5 %head_dft.1 = (bf16[256,16,128]{2,1,0:T(8,128)(2,1)}, f32[4,256,128]{2,1,0:T(8,128)S(1)}) custom-call(bf16[32,4096]{1,0:T(8,128)(2,1)S(1)} %slice.6.v_ref, bf16[32,3584]{1,0:T(8,128)(2,1)S(1)} %collective-permute-done.h_ref, f32[4,1792,128]{2,1,0:T(8,128)S(1)} %fir.1.f_ref, f32[8,512]{1,0:T(8,128)S(1)} %copy-done.11, bf16[256,512]{1,0:T(8,128)(2,1)S(1)} %copy-done.9), custom_call_target="tpu_custom_call" | custom-call | flops 536870912 | bytes 6291456 | tf_op jit(solution)/shard_map/head_dft/pallas_call | solution.py:187
  17.6 16.5 %all-to-all-start.1 = ((bf16[256,16,128]{2,1,0:T(8,128)(2,1)}), bf16[256,16,128]{2,1,0:T(8,128)(2,1)S(1)}, u32[]{:S(2)}, u32[]{:S(2)}) async-start(bf16[256,16,128]{2,1,0:T(8,128)(2,1)} %get-tuple-element.33), calls=%async_computation.1 | async-start | bytes 2097152 | tf_op jit(solution)/shard_map/all_to_all | solution.py:310
  34.1 2.0 %copy-done.1 = f32[4,1792,128]{2,1,0:T(8,128)S(1)} copy-done((f32[4,1792,128]{2,1,0:T(8,128)S(1)}, f32[4,1792,128]{2,1,0:T(8,128)}, u32[]{:S(2)}) %copy-start.1) | copy-done | bytes 3670040
  36.2 4.1 %dft.1 = bf16[256,16,128]{2,1,0:T(8,128)(2,1)} custom-call(f32[4,1792,128]{2,1,0:T(8,128)S(1)} %copy-done.1, f32[4,256,128]{2,1,0:T(8,128)S(1)} %get-tuple-element.32.head_ref, bf16[256,512]{1,0:T(8,128)(2,1)S(1)} %copy-done.10), custom_call_target="tpu_custom_call" | custom-call | flops 536870912 | bytes 6291456 | tf_op jit(solution)/shard_map/dft/pallas_call | solution.py:197
  40.3 26.5 %all-to-all-done.1.mine_ref = bf16[256,16,128]{2,1,0:T(8,128)(2,1)S(1)} async-done(((bf16[256,16,128]{2,1,0:T(8,128)(2,1)}), bf16[256,16,128]{2,1,0:T(8,128)(2,1)S(1)}, u32[]{:S(2)}, u32[]{:S(2)}) %all-to-all-start.1) | async-done | bytes 1048608 | tf_op jit(solution)/shard_map/all_to_all | solution.py:310
  66.7 5.2 %all-to-all-start = ((bf16[256,16,128]{2,1,0:T(8,128)(2,1)}), bf16[256,16,128]{2,1,0:T(8,128)(2,1)S(1)}, u32[]{:S(2)}, u32[]{:S(2)}) async-start(bf16[256,16,128]{2,1,0:T(8,128)(2,1)} %dft.1), calls=%async_computation | async-start | bytes 2097152 | tf_op jit(solution)/shard_map/all_to_all | solution.py:310
  73.6 2.2 %collective-permute-done.1.other_ref = bf16[256,16,128]{2,1,0:T(8,128)(2,1)S(1)} collective-permute-done((bf16[256,16,128]{2,1,0:T(8,128)(2,1)S(1)}, bf16[256,16,128]{2,1,0:T(8,128)(2,1)S(1)}, u32[]{:S(2)}, u32[]{:S(2)}) %collective-permute-start.1) | collective-permute-done | bytes 1048608 | tf_op jit(solution)/shard_map/ppermute | solution.py:316
  75.8 7.4 %correlate.2 = (bf16[2,128,512]{2,1,0:T(8,128)(2,1)S(1)}, bf16[2,128,512]{2,1,0:T(8,128)(2,1)S(1)}, bf16[2,128,512]{2,1,0:T(8,128)(2,1)S(1)}, bf16[2,128,512]{2,...) custom-call(s32[2]{0:T(128)S(1)} %pad_add_fusion.2.at_ref, ...), custom_call_target="tpu_custom_call" | custom-call | flops 2147483648 | bytes 8388608 | tf_op jit(solution)/shard_map/correlate/pallas_call | solution.py:253
  88.3 2.2 %collective-permute-start.6 = (bf16[2,128,512]{2,1,0:T(8,128)(2,1)}, bf16[2,128,512]{2,1,0:T(8,128)(2,1)S(1)}, u32[]{:S(2)}, u32[]{:S(2)}) collective-permute-start(bf16[2,128,512]{2,1,0:T(8,128)(2,1)} %get-tuple-element.38), channel_id=1, source_target_pairs={{0,4},{1,12},{2,6},{3,14},{4,0},{5,8},{6,2},{7,10},{8,5},{9,13},{1... | collective-permute-start | bytes 786440 | tf_op jit(solution)/shard_map/ppermute | solution.py:328
  90.6 7.3 %collective-permute-done.2.refs_0_ = bf16[2,128,512]{2,1,0:T(8,128)(2,1)S(1)} collective-permute-done((bf16[2,128,512]{2,1,0:T(8,128)(2,1)S(1)}, bf16[2,128,512]{2,1,0:T(8,128)(2,1)S(1)}, u32[]{:S(2)}, u32[]{:S(2)}) %collective-permute-start.2) | collective-permute-done | bytes 262176 | tf_op jit(solution)/shard_map/ppermute | solution.py:328
  97.9 2.7 %collective-permute-start.8 = (bf16[2,128,512]{2,1,0:T(8,128)(2,1)}, bf16[2,128,512]{2,1,0:T(8,128)(2,1)S(1)}, u32[]{:S(2)}, u32[]{:S(2)}) collective-permute-start(bf16[2,128,512]{2,1,0:T(8,128)(2,1)} %get-tuple-element.40), channel_id=1, source_target_pairs={{0,6},{1,14},{2,0},{3,8},{4,2},{5,10},{6,4},{7,12},{8,7},{9,15},{1... | collective-permute-start | bytes 786440 | tf_op jit(solution)/shard_map/ppermute | solution.py:328
  100.6 4.2 %collective-permute-done.4.refs_2_ = bf16[2,128,512]{2,1,0:T(8,128)(2,1)S(1)} collective-permute-done((bf16[2,128,512]{2,1,0:T(8,128)(2,1)S(1)}, bf16[2,128,512]{2,1,0:T(8,128)(2,1)S(1)}, u32[]{:S(2)}, u32[]{:S(2)}) %collective-permute-start.4) | collective-permute-done | bytes 262176 | tf_op jit(solution)/shard_map/ppermute | solution.py:328
  104.8 8.1 %collective-permute-start.9 = (bf16[2,128,512]{2,1,0:T(8,128)(2,1)}, bf16[2,128,512]{2,1,0:T(8,128)(2,1)S(1)}, u32[]{:S(2)}, u32[]{:S(2)}) collective-permute-start(bf16[2,128,512]{2,1,0:T(8,128)(2,1)} %get-tuple-element.41), channel_id=1, source_target_pairs={{0,7},{1,15},{2,1},{3,9},{4,3},{5,11},{6,5},{7,13},{8,6},{9,14},{1... | collective-permute-start | bytes 786440 | tf_op jit(solution)/shard_map/ppermute | solution.py:328
  114.8 4.2 %collective-permute-done.9.refs_7_ = bf16[2,128,512]{2,1,0:T(8,128)(2,1)S(1)} collective-permute-done((bf16[2,128,512]{2,1,0:T(8,128)(2,1)}, bf16[2,128,512]{2,1,0:T(8,128)(2,1)S(1)}, u32[]{:S(2)}, u32[]{:S(2)}) %collective-permute-start.9) | collective-permute-done | bytes 262176 | tf_op jit(solution)/shard_map/ppermute | solution.py:328
  119.0 5.3 %collective-permute-start.10 = (bf16[256,16,128]{2,1,0:T(8,128)(2,1)S(1)}, bf16[256,16,128]{2,1,0:T(8,128)(2,1)S(1)}, u32[]{:S(2)}, u32[]{:S(2)}) collective-permute-start(bf16[256,16,128]{2,1,0:T(8,128)(2,1)S(1)} %all-to-all-done.mine_ref), channel_id=1, source_target_pairs={{0,8},{8,0},{16,24},{24,16},{32,40},{40,32},{48,56},{56,48},{64,72... | collective-permute-start | bytes 3145736 | tf_op jit(solution)/shard_map/ppermute | solution.py:316
  124.3 2.3 %collective-permute-done.10.other_ref = bf16[256,16,128]{2,1,0:T(8,128)(2,1)S(1)} collective-permute-done((bf16[256,16,128]{2,1,0:T(8,128)(2,1)S(1)}, bf16[256,16,128]{2,1,0:T(8,128)(2,1)S(1)}, u32[]{:S(2)}, u32[]{:S(2)}) %collective-permute-start.10) | collective-permute-done | bytes 1048608 | tf_op jit(solution)/shard_map/ppermute | solution.py:316
  126.6 7.4 %correlate.3 = (bf16[2,128,512]{2,1,0:T(8,128)(2,1)S(1)}, bf16[2,128,512]{2,1,0:T(8,128)(2,1)S(1)}, bf16[2,128,512]{2,1,0:T(8,128)(2,1)S(1)}, bf16[2,128,512]{2,...) custom-call(s32[2]{0:T(128)S(1)} %pad_add_fusion.2.at_ref, ...), custom_call_target="tpu_custom_call" | custom-call | flops 2147483648 | bytes 8388608 | tf_op jit(solution)/shard_map/correlate/pallas_call | solution.py:253
  134.7 2.2 %collective-permute-start.13 = (bf16[2,128,512]{2,1,0:T(8,128)(2,1)S(1)}, bf16[2,128,512]{2,1,0:T(8,128)(2,1)S(1)}, u32[]{:S(2)}, u32[]{:S(2)}) collective-permute-start(bf16[2,128,512]{2,1,0:T(8,128)(2,1)S(1)} %get-tuple-element.53), channel_id=1, source_target_pairs={{0,10},{1,2},{2,12},{3,4},{4,14},{5,6},{6,8},{7,0},{8,11},{9,3},{1... | collective-permute-start | bytes 786440 | tf_op jit(solution)/shard_map/ppermute | solution.py:328
  136.9 4.6 %collective-permute-start.15 = (bf16[2,128,512]{2,1,0:T(8,128)(2,1)}, bf16[2,128,512]{2,1,0:T(8,128)(2,1)S(1)}, u32[]{:S(2)}, u32[]{:S(2)}) collective-permute-start(bf16[2,128,512]{2,1,0:T(8,128)(2,1)} %get-tuple-element.55), channel_id=1, source_target_pairs={{0,12},{1,4},{2,14},{3,6},{4,8},{5,0},{6,10},{7,2},{8,13},{9,5},{1... | collective-permute-start | bytes 786440 | tf_op jit(solution)/shard_map/ppermute | solution.py:328
  141.5 5.3 %collective-permute-start.17 = (bf16[2,128,512]{2,1,0:T(8,128)(2,1)}, bf16[2,128,512]{2,1,0:T(8,128)(2,1)S(1)}, u32[]{:S(2)}, u32[]{:S(2)}) collective-permute-start(bf16[2,128,512]{2,1,0:T(8,128)(2,1)} %get-tuple-element.57), channel_id=1, source_target_pairs={{0,14},{1,6},{2,8},{3,0},{4,10},{5,2},{6,12},{7,4},{8,15},{9,7},{1... | collective-permute-start | bytes 786440 | tf_op jit(solution)/shard_map/ppermute | solution.py:328
  146.9 11.4 %collective-permute-done.13.refs_3_ = bf16[2,128,512]{2,1,0:T(8,128)(2,1)S(1)} collective-permute-done((bf16[2,128,512]{2,1,0:T(8,128)(2,1)S(1)}, bf16[2,128,512]{2,1,0:T(8,128)(2,1)S(1)}, u32[]{:S(2)}, u32[]{:S(2)}) %collective-permute-start.13) | collective-permute-done | bytes 262176 | tf_op jit(solution)/shard_map/ppermute | solution.py:328
  161.4 4.2 %widen.2.refs_0_ = f32[8,2,256,512]{3,2,1,0:T(8,128)} custom-call(s32[2,8]{1,0:T(2,128)S(1)} %get-tuple-element.59.where_ref, bf16[2,128,512]{2,1,0:T(8,128)(2,1)S(1)} %collective-permute-done.2.refs_0_, bf16[2,128,512]{2,1,0:T(8,128)(2,1)S(1)} %collective-permute-done.3.refs_1_, bf16[2,128,512]{2,1,0:T(8,128)(2,1)S(1)} %collective-permute-done.4.refs_2_, ...), custom_call_target="tpu_custom_call" | custom-call | flops 1048576 | bytes 6291456 | tf_op jit(solution)/shard_map/widen/pallas_call | solution.py:283
  165.6 4.2 %widen.3 = f32[8,2,256,512]{3,2,1,0:T(8,128)} custom-call(s32[2,8]{1,0:T(2,128)S(1)} %get-tuple-element.60.where_ref, f32[8,2,256,512]{3,2,1,0:T(8,128)} %widen.2.refs_0_, bf16[2,128,512]{2,1,0:T(8,128)(2,1)S(1)} %collective-permute-done.11.refs_1_, bf16[2,128,512]{2,1,0:T(8,128)(2,1)S(1)} %collective-permute-done.12.refs_2_, ...), custom_call_target="tpu_custom_call", output_to_operand_aliasing={{}: (1, {})} | custom-call | flops 1048576 | bytes 6291456 | tf_op jit(solution)/shard_map/widen/pallas_call | solution.py:283
  (56 shorter events, 21.6 us)
Async XLA Ops:
  0.0 34.1 %copy-start.10 = (bf16[256,512]{1,0:T(8,128)(2,1)S(1)}, bf16[256,512]{1,0:T(8,128)(2,1)}, u32[]{:S(2)}) copy-start(bf16[256,512]{1,0:T(8,128)(2,1)} %constant.88.clone.tab_ref) | copy-start | bytes 786436
  1.0 9.3 %collective-permute-start = (bf16[32,3584]{1,0:T(8,128)(2,1)S(1)}, bf16[32,3584]{1,0:T(8,128)(2,1)S(1)}, u32[]{:S(2)}, u32[]{:S(2)}) collective-permute-start(bf16[32,3584]{1,0:T(8,128)(2,1)S(1)} %slice.7), channel_id=1, source_target_pairs={{0,1},{1,2},{2,3},{3,4},{4,5},{5,6},{6,7},{8,9},{9,10},{10,11},{11... | collective-permute-start | bytes 688136 | tf_op jit(solution)/shard_map/ppermute | solution.py:301
  17.6 49.1 %all-to-all-start.1 = ((bf16[256,16,128]{2,1,0:T(8,128)(2,1)}), bf16[256,16,128]{2,1,0:T(8,128)(2,1)S(1)}, u32[]{:S(2)}, u32[]{:S(2)}) async-start(bf16[256,16,128]{2,1,0:T(8,128)(2,1)} %get-tuple-element.33), calls=%async_computation.1 | async-start | bytes 2097152 | tf_op jit(solution)/shard_map/all_to_all | solution.py:310
  66.7 46.1 %all-to-all-start = ((bf16[256,16,128]{2,1,0:T(8,128)(2,1)}), bf16[256,16,128]{2,1,0:T(8,128)(2,1)S(1)}, u32[]{:S(2)}, u32[]{:S(2)}) async-start(bf16[256,16,128]{2,1,0:T(8,128)(2,1)} %dft.1), calls=%async_computation | async-start | bytes 2097152 | tf_op jit(solution)/shard_map/all_to_all | solution.py:310
  71.9 3.9 %collective-permute-start.1 = (bf16[256,16,128]{2,1,0:T(8,128)(2,1)S(1)}, bf16[256,16,128]{2,1,0:T(8,128)(2,1)S(1)}, u32[]{:S(2)}, u32[]{:S(2)}) collective-permute-start(bf16[256,16,128]{2,1,0:T(8,128)(2,1)S(1)} %all-to-all-done.1.mine_ref), channel_id=1, source_target_pairs={{0,8},{8,0},{16,24},{24,16},{32,40},{40,32},{48,56},{56,48},{64,72... | collective-permute-start | bytes 3145736 | tf_op jit(solution)/shard_map/ppermute | solution.py:316
  83.2 14.6 %collective-permute-start.2 = (bf16[2,128,512]{2,1,0:T(8,128)(2,1)S(1)}, bf16[2,128,512]{2,1,0:T(8,128)(2,1)S(1)}, u32[]{:S(2)}, u32[]{:S(2)}) collective-permute-start(bf16[2,128,512]{2,1,0:T(8,128)(2,1)S(1)} %get-tuple-element.34), channel_id=1, source_target_pairs={{0,0},{1,8},{2,2},{3,10},{4,4},{5,12},{6,6},{7,14},{8,1},{9,9},{10... | collective-permute-start | bytes 786440 | tf_op jit(solution)/shard_map/ppermute | solution.py:328
  85.2 12.7 %collective-permute-start.3 = (bf16[2,128,512]{2,1,0:T(8,128)(2,1)S(1)}, bf16[2,128,512]{2,1,0:T(8,128)(2,1)S(1)}, u32[]{:S(2)}, u32[]{:S(2)}) collective-permute-start(bf16[2,128,512]{2,1,0:T(8,128)(2,1)S(1)} %get-tuple-element.35), channel_id=1, source_target_pairs={{0,1},{1,9},{2,3},{3,11},{4,5},{5,13},{6,7},{7,15},{8,0},{9,8},{10... | collective-permute-start | bytes 786440 | tf_op jit(solution)/shard_map/ppermute | solution.py:328
  85.3 19.5 %collective-permute-start.4 = (bf16[2,128,512]{2,1,0:T(8,128)(2,1)S(1)}, bf16[2,128,512]{2,1,0:T(8,128)(2,1)S(1)}, u32[]{:S(2)}, u32[]{:S(2)}) collective-permute-start(bf16[2,128,512]{2,1,0:T(8,128)(2,1)S(1)} %get-tuple-element.36), channel_id=1, source_target_pairs={{0,2},{1,10},{2,4},{3,12},{4,6},{5,14},{6,0},{7,8},{8,3},{9,11},{1... | collective-permute-start | bytes 786440 | tf_op jit(solution)/shard_map/ppermute | solution.py:328
  86.4 26.5 %collective-permute-start.5 = (bf16[2,128,512]{2,1,0:T(8,128)(2,1)}, bf16[2,128,512]{2,1,0:T(8,128)(2,1)S(1)}, u32[]{:S(2)}, u32[]{:S(2)}) collective-permute-start(bf16[2,128,512]{2,1,0:T(8,128)(2,1)} %get-tuple-element.37), channel_id=1, source_target_pairs={{0,3},{1,11},{2,5},{3,13},{4,7},{5,15},{6,1},{7,9},{8,2},{9,10},{1... | collective-permute-start | bytes 786440 | tf_op jit(solution)/shard_map/ppermute | solution.py:328
  88.3 24.6 %collective-permute-start.6 = (bf16[2,128,512]{2,1,0:T(8,128)(2,1)}, bf16[2,128,512]{2,1,0:T(8,128)(2,1)S(1)}, u32[]{:S(2)}, u32[]{:S(2)}) collective-permute-start(bf16[2,128,512]{2,1,0:T(8,128)(2,1)} %get-tuple-element.38), channel_id=1, source_target_pairs={{0,4},{1,12},{2,6},{3,14},{4,0},{5,8},{6,2},{7,10},{8,5},{9,13},{1... | collective-permute-start | bytes 786440 | tf_op jit(solution)/shard_map/ppermute | solution.py:328
  97.9 16.6 %collective-permute-start.7 = (bf16[2,128,512]{2,1,0:T(8,128)(2,1)}, bf16[2,128,512]{2,1,0:T(8,128)(2,1)S(1)}, u32[]{:S(2)}, u32[]{:S(2)}) collective-permute-start(bf16[2,128,512]{2,1,0:T(8,128)(2,1)} %get-tuple-element.39), channel_id=1, source_target_pairs={{0,5},{1,13},{2,7},{3,15},{4,1},{5,9},{6,3},{7,11},{8,4},{9,12},{1... | collective-permute-start | bytes 786440 | tf_op jit(solution)/shard_map/ppermute | solution.py:328
  97.9 16.9 %collective-permute-start.8 = (bf16[2,128,512]{2,1,0:T(8,128)(2,1)}, bf16[2,128,512]{2,1,0:T(8,128)(2,1)S(1)}, u32[]{:S(2)}, u32[]{:S(2)}) collective-permute-start(bf16[2,128,512]{2,1,0:T(8,128)(2,1)} %get-tuple-element.40), channel_id=1, source_target_pairs={{0,6},{1,14},{2,0},{3,8},{4,2},{5,10},{6,4},{7,12},{8,7},{9,15},{1... | collective-permute-start | bytes 786440 | tf_op jit(solution)/shard_map/ppermute | solution.py:328
  104.8 14.2 %collective-permute-start.9 = (bf16[2,128,512]{2,1,0:T(8,128)(2,1)}, bf16[2,128,512]{2,1,0:T(8,128)(2,1)S(1)}, u32[]{:S(2)}, u32[]{:S(2)}) collective-permute-start(bf16[2,128,512]{2,1,0:T(8,128)(2,1)} %get-tuple-element.41), channel_id=1, source_target_pairs={{0,7},{1,15},{2,1},{3,9},{4,3},{5,11},{6,5},{7,13},{8,6},{9,14},{1... | collective-permute-start | bytes 786440 | tf_op jit(solution)/shard_map/ppermute | solution.py:328
  114.8 26.7 %copy-start.5 = (bf16[2,128,512]{2,1,0:T(8,128)(2,1)}, bf16[2,128,512]{2,1,0:T(8,128)(2,1)S(1)}, u32[]{:S(2)}) copy-start(bf16[2,128,512]{2,1,0:T(8,128)(2,1)S(1)} %collective-permute-done.8.refs_6_) | copy-start | bytes 786436
  119.0 22.6 %copy-start.7 = (bf16[2,128,512]{2,1,0:T(8,128)(2,1)}, bf16[2,128,512]{2,1,0:T(8,128)(2,1)S(1)}, u32[]{:S(2)}) copy-start(bf16[2,128,512]{2,1,0:T(8,128)(2,1)S(1)} %collective-permute-done.9.refs_7_) | copy-start | bytes 786436
  119.0 7.6 %collective-permute-start.10 = (bf16[256,16,128]{2,1,0:T(8,128)(2,1)S(1)}, bf16[256,16,128]{2,1,0:T(8,128)(2,1)S(1)}, u32[]{:S(2)}, u32[]{:S(2)}) collective-permute-start(bf16[256,16,128]{2,1,0:T(8,128)(2,1)S(1)} %all-to-all-done.mine_ref), channel_id=1, source_target_pairs={{0,8},{8,0},{16,24},{24,16},{32,40},{40,32},{48,56},{56,48},{64,72... | collective-permute-start | bytes 3145736 | tf_op jit(solution)/shard_map/ppermute | solution.py:316
  134.0 7.5 %collective-permute-start.11 = (bf16[2,128,512]{2,1,0:T(8,128)(2,1)S(1)}, bf16[2,128,512]{2,1,0:T(8,128)(2,1)S(1)}, u32[]{:S(2)}, u32[]{:S(2)}) collective-permute-start(bf16[2,128,512]{2,1,0:T(8,128)(2,1)S(1)} %get-tuple-element.51), channel_id=1, source_target_pairs={{0,8},{1,0},{2,10},{3,2},{4,12},{5,4},{6,14},{7,6},{8,9},{9,1},{10... | collective-permute-start | bytes 786440 | tf_op jit(solution)/shard_map/ppermute | solution.py:328
  134.0 7.5 %collective-permute-start.12 = (bf16[2,128,512]{2,1,0:T(8,128)(2,1)S(1)}, bf16[2,128,512]{2,1,0:T(8,128)(2,1)S(1)}, u32[]{:S(2)}, u32[]{:S(2)}) collective-permute-start(bf16[2,128,512]{2,1,0:T(8,128)(2,1)S(1)} %get-tuple-element.52), channel_id=1, source_target_pairs={{0,9},{1,1},{2,11},{3,3},{4,13},{5,5},{6,15},{7,7},{8,8},{9,0},{10... | collective-permute-start | bytes 786440 | tf_op jit(solution)/shard_map/ppermute | solution.py:328
  134.7 23.6 %collective-permute-start.13 = (bf16[2,128,512]{2,1,0:T(8,128)(2,1)S(1)}, bf16[2,128,512]{2,1,0:T(8,128)(2,1)S(1)}, u32[]{:S(2)}, u32[]{:S(2)}) collective-permute-start(bf16[2,128,512]{2,1,0:T(8,128)(2,1)S(1)} %get-tuple-element.53), channel_id=1, source_target_pairs={{0,10},{1,2},{2,12},{3,4},{4,14},{5,6},{6,8},{7,0},{8,11},{9,3},{1... | collective-permute-start | bytes 786440 | tf_op jit(solution)/shard_map/ppermute | solution.py:328
  136.9 28.6 %collective-permute-start.14 = (bf16[2,128,512]{2,1,0:T(8,128)(2,1)}, bf16[2,128,512]{2,1,0:T(8,128)(2,1)S(1)}, u32[]{:S(2)}, u32[]{:S(2)}) collective-permute-start(bf16[2,128,512]{2,1,0:T(8,128)(2,1)} %get-tuple-element.54), channel_id=1, source_target_pairs={{0,11},{1,3},{2,13},{3,5},{4,15},{5,7},{6,9},{7,1},{8,10},{9,2},{1... | collective-permute-start | bytes 786440 | tf_op jit(solution)/shard_map/ppermute | solution.py:328
  136.9 28.6 %collective-permute-start.15 = (bf16[2,128,512]{2,1,0:T(8,128)(2,1)}, bf16[2,128,512]{2,1,0:T(8,128)(2,1)S(1)}, u32[]{:S(2)}, u32[]{:S(2)}) collective-permute-start(bf16[2,128,512]{2,1,0:T(8,128)(2,1)} %get-tuple-element.55), channel_id=1, source_target_pairs={{0,12},{1,4},{2,14},{3,6},{4,8},{5,0},{6,10},{7,2},{8,13},{9,5},{1... | collective-permute-start | bytes 786440 | tf_op jit(solution)/shard_map/ppermute | solution.py:328
  141.5 24.0 %collective-permute-start.16 = (bf16[2,128,512]{2,1,0:T(8,128)(2,1)}, bf16[2,128,512]{2,1,0:T(8,128)(2,1)S(1)}, u32[]{:S(2)}, u32[]{:S(2)}) collective-permute-start(bf16[2,128,512]{2,1,0:T(8,128)(2,1)} %get-tuple-element.56), channel_id=1, source_target_pairs={{0,13},{1,5},{2,15},{3,7},{4,9},{5,1},{6,11},{7,3},{8,12},{9,4},{1... | collective-permute-start | bytes 786440 | tf_op jit(solution)/shard_map/ppermute | solution.py:328
  141.5 24.0 %collective-permute-start.17 = (bf16[2,128,512]{2,1,0:T(8,128)(2,1)}, bf16[2,128,512]{2,1,0:T(8,128)(2,1)S(1)}, u32[]{:S(2)}, u32[]{:S(2)}) collective-permute-start(bf16[2,128,512]{2,1,0:T(8,128)(2,1)} %get-tuple-element.57), channel_id=1, source_target_pairs={{0,14},{1,6},{2,8},{3,0},{4,10},{5,2},{6,12},{7,4},{8,15},{9,7},{1... | collective-permute-start | bytes 786440 | tf_op jit(solution)/shard_map/ppermute | solution.py:328
  158.3 7.3 %collective-permute-start.18 = (bf16[2,128,512]{2,1,0:T(8,128)(2,1)}, bf16[2,128,512]{2,1,0:T(8,128)(2,1)S(1)}, u32[]{:S(2)}, u32[]{:S(2)}) collective-permute-start(bf16[2,128,512]{2,1,0:T(8,128)(2,1)} %get-tuple-element.58), channel_id=1, source_target_pairs={{0,15},{1,7},{2,9},{3,1},{4,11},{5,3},{6,13},{7,5},{8,14},{9,6},{1... | collective-permute-start | bytes 786440 | tf_op jit(solution)/shard_map/ppermute | solution.py:328
  (9 other events, 32.5 us)

commit v3 on v2

--- a/solution.py
+++ b/solution.py
@@ -7,6 +7,7 @@
 from jax import lax
 from jax.experimental import pallas as pl
 from jax.experimental.pallas import tpu as pltpu
+from jax.sharding import Mesh
 from jax.sharding import PartitionSpec as P
 
 FFT_LEN = 512
@@ -16,7 +17,8 @@
 CORES = 2
 HEAD = 8
 CHUNKS = FFT_LEN // LANES
-ALL = ("chan", "row", "col")
+CHIPS = ("pair", "row", "col")
+ALL = ("pair", "core", "row", "col")
 VMEM = pl.BlockSpec(memory_space=pltpu.VMEM)
 SMEM = pl.BlockSpec(memory_space=pltpu.SMEM)
 NT = (((1,), (1,)), ((), ()))
@@ -97,7 +99,7 @@
 
 
 def dft(f_ref, head_ref, tab_ref, o_ref, t_ref):
-    inputs = o_ref.shape[1] * CORES
+    inputs = o_ref.shape[1]
     channels = tab_ref.shape[0] // 2
     body_len = f_ref.shape[1] // inputs
     spectra = body_len + HEAD
@@ -127,18 +129,15 @@
 
     lax.fori_loop(0, inputs // group, transform, 0)
 
-    half = inputs // CORES
-    slots = 8
-
-    def cast(pair, carry):
-        for core in range(CORES):
-            for slot in range(slots):
-                first = pl.multiple_of((pair * slots + slot) * inputs + core * half, half)
-                rows = t_ref[pl.ds(first, half), :]
-                o_ref[pair * (CORES * slots) + core * slots + slot] = rows.astype(jnp.bfloat16)
+    step = 8
+
+    def cast(index, carry):
+        for j in range(step):
+            first = pl.multiple_of((index * step + j) * inputs, inputs)
+            o_ref[index * step + j] = t_ref[pl.ds(first, inputs), :].astype(jnp.bfloat16)
         return carry
 
-    lax.fori_loop(0, channels // slots, cast, 0)
+    lax.fori_loop(0, channels // step, cast, 0)
 
 
 def head_kernel(v_ref, h_ref, f_ref, w_ref, tab_ref, o_ref, head_ref, t_ref):
@@ -157,7 +156,7 @@
     dft(f_ref, head_ref, tab_ref, o_ref, t_ref)
 
 
-def params(mib=24):
+def params(mib=12):
     return pltpu.CompilerParams(vmem_limit_bytes=mib << 20)
 
 
@@ -181,7 +180,7 @@
         cost_estimate=cost(16 * voltages.size, 6 * voltages.size),
         name="fir",
     )(voltages, window)
-    message = jax.ShapeDtypeStruct((CHANNELS, inputs // CORES, 2 * spectra), jnp.bfloat16)
+    message = jax.ShapeDtypeStruct((channels, inputs, 2 * spectra), jnp.bfloat16)
     scratch = [pltpu.VMEM((channels * inputs, 2 * spectra), jnp.float32)]
     work = cost(4 * channels * FFT_LEN * inputs * spectra, 6 * voltages.size)
     first, head = pl.pallas_call(
@@ -207,88 +206,92 @@
     return first, second
 
 
-def correlate_kernel(groups, rows, cols, scale, at_ref, mine_ref, other_ref, *refs):
-    outs, (x_ref, y_ref) = refs[:-2], refs[-2:]
+def correlate_kernel(pairs, rows, cols, scale, at_ref, mine_ref, other_ref, *refs):
+    outs, (x_ref, l_ref) = refs[:-2], refs[-2:]
     core, row = at_ref[0], at_ref[1]
-    part = mine_ref.shape[1]
-    height = CORES * part
+    height = mine_ref.shape[1]
     slots = rows * cols
     half = LANES // 2
 
-    def place(g, carry):
+    def place(pair, carry):
         for ref, owner in ((mine_ref, core), (other_ref, 1 - core)):
-            dest = pl.ds(pl.multiple_of(g * height + owner * part, part), part)
+            dest = pl.ds(pl.multiple_of((pair * CORES + owner) * height, height), height)
             for t in range(slots):
-                x_ref[dest, t * LANES : (t + 1) * LANES] = ref[g * slots + t]
+                x_ref[dest, t * LANES : (t + 1) * LANES] = ref[pair * slots + t]
         return carry
 
-    lax.fori_loop(0, groups, place, 0)
-
-    row_block = groups * height // rows
-    row_half = row_block // CORES
-    col_block = groups * height // cols
-    upper = lax.broadcasted_iota(jnp.int32, (row_half, LANES), 1) >= half
+    lax.fori_loop(0, pairs, place, 0)
+
+    row_block = x_ref.shape[0] // rows
+    part = row_block // CORES
+    col_block = x_ref.shape[0] // cols
+    upper = lax.broadcasted_iota(jnp.int32, (part, LANES), 1) >= half
     for dy in range(rows):
-        first = pl.multiple_of(lax.rem(row + dy, rows) * row_block + core * row_half, row_half)
-        left = pl.ds(first, row_half)
+        first = pl.multiple_of(lax.rem(row + dy, rows) * row_block + core * part, part)
+        left = pl.ds(first, part)
         for t in range(slots):
             lanes = slice(t * LANES, (t + 1) * LANES)
-            turned = pltpu.roll(x_ref[left, lanes].astype(jnp.float32), half, 1)
-            y_ref[:, lanes] = jnp.where(upper, -turned, turned).astype(jnp.bfloat16)
-        for d in range(cols):
-            col = jnp.bitwise_xor(core, d)
-            right = x_ref[pl.ds(pl.multiple_of(col * col_block, col_block), col_block), :]
-            real = lax.dot_general(x_ref[left, :], right, NT, preferred_element_type=jnp.float32)
-            imag = lax.dot_general(y_ref[...], right, NT, preferred_element_type=jnp.float32)
-            out = outs[dy * cols + d]
-            out[0] = (real * scale).astype(jnp.bfloat16)
-            out[1] = (imag * scale).astype(jnp.bfloat16)
-
-
-def correlate(at, mine, other, groups, rows, cols, scale):
-    total = groups * mine.shape[1] * CORES
+            value = x_ref[left, lanes]
+            turned = pltpu.roll(value.astype(jnp.float32), half, 1)
+            l_ref[2 * dy * part : (2 * dy + 1) * part, lanes] = value
+            l_ref[(2 * dy + 1) * part : (2 * dy + 2) * part, lanes] = jnp.where(upper, -turned, turned).astype(jnp.bfloat16)
+    joint = 2
+    for d in range(cols):
+        col = jnp.bitwise_xor(core, d)
+        right = x_ref[pl.ds(pl.multiple_of(col * col_block, col_block), col_block), :]
+        for dy in range(0, rows, joint):
+            left = l_ref[2 * dy * part : 2 * (dy + joint) * part, :]
+            value = lax.dot_general(left, right, NT, preferred_element_type=jnp.float32) * scale
+            for j in range(joint):
+                for p in range(2):
+                    outs[(dy + j) * cols + d][p] = value[(2 * j + p) * part : (2 * j + p + 1) * part].astype(jnp.bfloat16)
+
+
+def correlate(at, mine, other, pairs, rows, cols, scale):
+    total = pairs * mine.shape[1] * CORES
     depth = rows * cols * LANES
     row_half, col_block = total // rows // CORES, total // cols
     piece = jax.ShapeDtypeStruct((2, row_half, col_block), jnp.bfloat16)
     return pl.pallas_call(
-        functools.partial(correlate_kernel, groups, rows, cols, scale),
+        functools.partial(correlate_kernel, pairs, rows, cols, scale),
         out_shape=[piece] * (rows * cols),
         in_specs=[SMEM, VMEM, VMEM],
         out_specs=[VMEM] * (rows * cols),
-        scratch_shapes=[pltpu.VMEM((total, depth), jnp.bfloat16), pltpu.VMEM((row_half, depth), jnp.bfloat16)],
+        scratch_shapes=[pltpu.VMEM((total, depth), jnp.bfloat16), pltpu.VMEM((2 * rows * row_half, depth), jnp.bfloat16)],
         compiler_params=params(),
         cost_estimate=cost(2 * total * total * depth, 8 * total * depth),
         name="correlate",
     )(at, mine, other)
 
 
-def widen_kernel(count, aliased, where_ref, *refs):
-    o_ref = refs[-1]
-    for j in range(count):
-
-        @pl.when(pl.program_id(0) == j)
-        def _():
-            o_ref[0] = refs[aliased + j][...].astype(jnp.float32)
+def widen_kernel(count, where_ref, *refs):
+    pieces, o_ref, wide_ref, sems = refs[-count - 3 : -3], refs[-3], refs[-2], refs[-1]
+    height = pieces[0].shape[1]
+    copies = []
+    for j, piece in enumerate(pieces):
+        wide_ref[j] = piece[...].astype(jnp.float32)
+        rows = pl.ds(pl.multiple_of(where_ref[1, j] * height, height), height)
+        copies.append(pltpu.make_async_copy(wide_ref.at[j], o_ref.at[where_ref[0, j], :, rows, :], sems.at[j]))
+        copies[-1].start()
+    for copy in copies:
+        copy.wait()
 
 
 def widen(pieces, where, shape, into=None):
-    _, row_half, col_block = pieces[0].shape
-    aliased = 0 if into is None else 1
-    spec = pltpu.PrefetchScalarGridSpec(
-        num_scalar_prefetch=1,
-        grid=(len(pieces),),
-        in_specs=[pl.BlockSpec(memory_space=pl.ANY)] * aliased + [VMEM] * len(pieces),
-        out_specs=pl.BlockSpec((1, 2, row_half, col_block), lambda j, at: (at[0, j], 0, at[1, j], 0)),
-    )
+    count, piece = len(pieces), pieces[0]
+    before = [] if into is None else [into]
+    anywhere = pl.BlockSpec(memory_space=pl.ANY)
     return pl.pallas_call(
-        functools.partial(widen_kernel, len(pieces), aliased),
-        grid_spec=spec,
+        functools.partial(widen_kernel, count),
+        in_specs=[SMEM] + [anywhere] * len(before) + [VMEM] * count,
+        out_specs=anywhere,
         out_shape=jax.ShapeDtypeStruct(shape, jnp.float32),
-        input_output_aliases={1: 0} if aliased else {},
-        compiler_params=params(),
-        cost_estimate=cost(len(pieces) * pieces[0].size, 6 * len(pieces) * pieces[0].size),
+        scratch_shapes=[pltpu.VMEM((count, *piece.shape), jnp.float32), pltpu.SemaphoreType.DMA((count,))],
+        input_output_aliases={1: 0} if before else {},
+        compiler_params=params(8),
+        cost_estimate=cost(count * piece.size, 6 * count * piece.size),
         name="widen",
-    )(where, *([] if into is None else [into]), *pieces)
+    )(where, *before, *pieces)
 
 
 def per_device(voltages):
@@ -296,36 +299,35 @@
     rows = lax.axis_size("row")
     cols = lax.axis_size("col")
     slots = rows * cols
-    groups = lax.axis_size("chan")
+    pairs = lax.axis_size("pair")
     tail = voltages[:, (slot_spectra - TAPS + 1) * FFT_LEN :]
     earlier = lax.ppermute(tail, ("row", "col"), [(i, i + 1) for i in range(slots - 1)])
-    core = lax.axis_index("chan") % CORES
+    core = lax.axis_index("core")
     row, col = lax.axis_index("row"), lax.axis_index("col")
     at = jnp.stack([core, row]).astype(jnp.int32)
     scale = 1.0 / (slot_spectra * slots)
-    total = groups * voltages.shape[0]
+    total = pairs * CORES * voltages.shape[0]
     shape = (slots, 2, total // rows, total // cols)
     messages = channelize(voltages, earlier, rows, cols)
-    swap = [(i, i ^ 1) for i in range(groups)]
-    arrived = [lax.all_to_all(message, ALL, split_axis=0, concat_axis=0, tiled=True) for message in messages]
+    arrived = [lax.all_to_all(message, CHIPS, split_axis=0, concat_axis=0, tiled=True) for message in messages]
     out = None
     for chunk, mine in enumerate(arrived):
         if chunk:
             mine, got = lax.optimization_barrier((mine, got))
             out = widen(got, where, shape)
-        other = lax.ppermute(mine, "chan", swap)
-        sent = correlate(at, mine, other, groups, rows, cols, scale)
+        other = lax.ppermute(mine, "core", [(0, 1), (1, 0)])
+        sent = correlate(at, mine, other, pairs, rows, cols, scale)
         got, channel, half = [], [], []
         for dy in range(rows):
             for d in range(cols):
-                pairs = []
-                for c in range(groups):
+                links = []
+                for c in range(pairs * CORES):
                     for r in range(rows):
                         for x in range(cols):
                             to_core = x if chunk == 0 else 1 - x
                             target = (c - c % CORES + to_core, (r + dy) % rows, (c % CORES) ^ d)
-                            pairs.append(((c * rows + r) * cols + x, (target[0] * rows + target[1]) * cols + target[2]))
-                got.append(lax.ppermute(sent[dy * cols + d], ALL, pairs))
+                            links.append(((c * rows + r) * cols + x, (target[0] * rows + target[1]) * cols + target[2]))
+                got.append(lax.ppermute(sent[dy * cols + d], ALL, links))
                 from_col = core if chunk == 0 else 1 - core
                 channel.append((row + rows - dy) % rows * cols + from_col)
                 half.append(jnp.bitwise_xor(col, d))
@@ -334,11 +336,12 @@
 
 
 def solution(mesh):
-    placed = (P("chan", ("row", "col")),)
+    groups, rows, cols = mesh.devices.shape
+    finer = Mesh(mesh.devices.reshape(groups // CORES, CORES, rows, cols), ALL)
     return jax.shard_map(
         per_device,
-        mesh=mesh,
-        in_specs=placed,
-        out_specs=P("chan", None, "row", "col"),
+        mesh=finer,
+        in_specs=(P(("pair", "core"), ("row", "col")),),
+        out_specs=P(("pair", "core"), None, "row", "col"),
         check_vma=False,
     )

time: 170 us -> 159 us (0.935)
  Pallas kernels: 33.8 us -> 24.2 us
  waiting for transfers between devices: 60 us -> 55.6 us
  starting transfers between devices: 63.5 us -> 66.3 us
    pallas_call x4, Pallas kernels: 23.1 us -> 13.5 us  [the longest x2 8.24 us: correlate(): pl.pallas_call(functools.partial(correlate_kernel, pairs, rows, cols, sca...]
    all_to_all x2, waiting for transfers between devices: 26.5 us -> 20 us  [per_device(): lax.all_to_all(message, CHIPS, split_axis=0, concat_axis=0, tiled=True)]
    all_to_all x2, starting transfers between devices: 21.7 us -> 26.2 us  [per_device(): lax.all_to_all(message, CHIPS, split_axis=0, concat_axis=0, tiled=True)]
    ppermute x18, waiting for transfers between devices: 33.5 us -> 35.6 us  [the longest x16 31.1 us: per_device(): got.append(lax.ppermute(sent[dy * cols + d], ALL, links))]
    ppermute x18, starting transfers between devices: 37.9 us -> 36.1 us  [the longest x16 33.2 us: per_device(): got.append(lax.ppermute(sent[dy * cols + d], ALL, links))]
  transfers between devices with their start and end apart: 21 -> 21, of which waited for: 9 -> 13; matrix products, arithmetic and copies ran while one was open for 1% -> 1% of each run, Pallas kernels for 10% -> 8%
where the time goes in v3:
time: 159 us
  starting transfers between devices  66.3 us (42%)
  waiting for transfers between devices  55.6 us (35%)
  Pallas kernels  24.2 us (15%)
  local copies, waits for them, and re-layouts  12.2 us (8%)
    ppermute x16, starting transfers between devices, per_device(): got.append(lax.ppermute(sent[dy * cols + d], ALL, links))  33.2 us
    ppermute x16, waiting for transfers between devices, per_device(): got.append(lax.ppermute(sent[dy * cols + d], ALL, links))  31.1 us
    all_to_all x2, starting transfers between devices, per_device(): lax.all_to_all(message, CHIPS, split_axis=0, concat_axis=0, tiled=True)  26.2 us
    all_to_all x2, waiting for transfers between devices, per_device(): lax.all_to_all(message, CHIPS, split_axis=0, concat_axis=0, tiled=True)  20 us
    unnamed x24, local copies, waits for them, and re-layouts  9.98 us
    pallas_call x2, Pallas kernels, correlate(): pl.pallas_call(functools.partial(correlate_kernel, pairs, rows, cols, sca...  8.24 us
    pallas_call x2, Pallas kernels, widen(): pl.pallas_call(functools.partial(widen_kernel, count), in_specs=[SMEM] +...  5.3 us
    pallas_call x1, Pallas kernels, channelize(): pl.pallas_call(head_kernel, out_shape=[message, jax.ShapeDtypeStruct((CHU...  4.51 us
  transfers between devices with their start and end apart: 21, of which 13 were waited for; matrix products, arithmetic and copies ran while one was open for 1% of the time, Pallas kernels for 8%

profile of v3, /device:TPU:1, one launch (start us, length us, event | category | flops | bytes accessed | tf_op | source)
XLA Modules:
  0.0 158.7 jit_solution(11073378461597383303)
XLA Ops:
  1.0 4.0 %collective-permute-start = (bf16[32,3584]{1,0:T(8,128)(2,1)S(1)}, bf16[32,3584]{1,0:T(8,128)(2,1)S(1)}, u32[]{:S(2)}, u32[]{:S(2)}) collective-permute-start(bf16[32,3584]{1,0:T(8,128)(2,1)S(1)} %slice.7), channel_id=1, source_target_pairs={{0,1},{1,2},{2,3},{3,4},{4,5},{5,6},{6,7},{8,9},{9,10},{10,11},{11... | collective-permute-start | bytes 688136 | tf_op jit(solution)/shard_map/ppermute | solution.py:304
  11.2 4.5 %head_dft.1 = (bf16[128,32,128]{2,1,0:T(8,128)(2,1)}, f32[4,256,128]{2,1,0:T(8,128)S(1)}) custom-call(bf16[32,4096]{1,0:T(8,128)(2,1)S(1)} %slice.6.v_ref, bf16[32,3584]{1,0:T(8,128)(2,1)S(1)} %collective-permute-done.h_ref, f32[4,1792,128]{2,1,0:T(8,128)S(1)} %fir.1.f_ref, f32[8,512]{1,0:T(8,128)S(1)} %copy-done.11, bf16[256,512]{1,0:T(8,128)(2,1)S(1)} %copy-done.9), custom_call_target="tpu_custom_call" | custom-call | flops 536870912 | bytes 6291456 | tf_op jit(solution)/shard_map/head_dft/pallas_call | solution.py:186
  17.6 16.3 %all-to-all-start.1 = ((bf16[128,32,128]{2,1,0:T(8,128)(2,1)}), bf16[128,32,128]{2,1,0:T(8,128)(2,1)S(1)}, u32[]{:S(2)}, u32[]{:S(2)}) async-start(bf16[128,32,128]{2,1,0:T(8,128)(2,1)} %get-tuple-element.33), calls=%async_computation.1 | async-start | bytes 2097152 | tf_op jit(solution)/shard_map/all_to_all | solution.py:312
  36.0 4.1 %dft.1 = bf16[128,32,128]{2,1,0:T(8,128)(2,1)} custom-call(f32[4,1792,128]{2,1,0:T(8,128)S(1)} %copy-done.1, f32[4,256,128]{2,1,0:T(8,128)S(1)} %get-tuple-element.32.head_ref, bf16[256,512]{1,0:T(8,128)(2,1)S(1)} %copy-done.10), custom_call_target="tpu_custom_call" | custom-call | flops 536870912 | bytes 6291456 | tf_op jit(solution)/shard_map/dft/pallas_call | solution.py:196
  40.1 20.0 %all-to-all-done.1.mine_ref = bf16[128,32,128]{2,1,0:T(8,128)(2,1)S(1)} async-done(((bf16[128,32,128]{2,1,0:T(8,128)(2,1)}), bf16[128,32,128]{2,1,0:T(8,128)(2,1)S(1)}, u32[]{:S(2)}, u32[]{:S(2)}) %all-to-all-start.1) | async-done | bytes 1048608 | tf_op jit(solution)/shard_map/all_to_all | solution.py:312
  60.1 9.9 %all-to-all-start = ((bf16[128,32,128]{2,1,0:T(8,128)(2,1)}), bf16[128,32,128]{2,1,0:T(8,128)(2,1)S(1)}, u32[]{:S(2)}, u32[]{:S(2)}) async-start(bf16[128,32,128]{2,1,0:T(8,128)(2,1)} %dft.1), calls=%async_computation | async-start | bytes 2097152 | tf_op jit(solution)/shard_map/all_to_all | solution.py:312
  70.0 2.4 %collective-permute-start.1 = (bf16[128,32,128]{2,1,0:T(8,128)(2,1)S(1)}, bf16[128,32,128]{2,1,0:T(8,128)(2,1)S(1)}, u32[]{:S(2)}, u32[]{:S(2)}) collective-permute-start(bf16[128,32,128]{2,1,0:T(8,128)(2,1)S(1)} %all-to-all-done.1.mine_ref), channel_id=1, source_target_pairs={{0,8},{8,0},{1,9},{9,1},{2,10},{10,2},{3,11},{11,3},{4,12},{12,4},... | collective-permute-start | bytes 3145736 | tf_op jit(solution)/shard_map/ppermute | solution.py:318
  74.7 4.1 %correlate.2 = (bf16[2,128,512]{2,1,0:T(8,128)(2,1)S(1)}, bf16[2,128,512]{2,1,0:T(8,128)(2,1)S(1)}, bf16[2,128,512]{2,1,0:T(8,128)(2,1)S(1)}, bf16[2,128,512]{2,...) custom-call(s32[2]{0:T(128)S(1)} %pad_add_fusion.2.at_ref, ...), custom_call_target="tpu_custom_call" | custom-call | flops 2147483648 | bytes 8388608 | tf_op jit(solution)/shard_map/correlate/pallas_call | solution.py:255
  78.8 3.0 %collective-permute-start.2 = (bf16[2,128,512]{2,1,0:T(8,128)(2,1)S(1)}, bf16[2,128,512]{2,1,0:T(8,128)(2,1)S(1)}, u32[]{:S(2)}, u32[]{:S(2)}) collective-permute-start(bf16[2,128,512]{2,1,0:T(8,128)(2,1)S(1)} %get-tuple-element.34), channel_id=1, source_target_pairs={{0,0},{1,8},{2,2},{3,10},{4,4},{5,12},{6,6},{7,14},{8,1},{9,9},{10... | collective-permute-start | bytes 786440 | tf_op jit(solution)/shard_map/ppermute | solution.py:330
  87.3 6.0 %collective-permute-done.2.refs_0_ = bf16[2,128,512]{2,1,0:T(8,128)(2,1)S(1)} collective-permute-done((bf16[2,128,512]{2,1,0:T(8,128)(2,1)S(1)}, bf16[2,128,512]{2,1,0:T(8,128)(2,1)S(1)}, u32[]{:S(2)}, u32[]{:S(2)}) %collective-permute-start.2) | collective-permute-done | bytes 262176 | tf_op jit(solution)/shard_map/ppermute | solution.py:330
  94.4 3.3 %collective-permute-start.8 = (bf16[2,128,512]{2,1,0:T(8,128)(2,1)}, bf16[2,128,512]{2,1,0:T(8,128)(2,1)S(1)}, u32[]{:S(2)}, u32[]{:S(2)}) collective-permute-start(bf16[2,128,512]{2,1,0:T(8,128)(2,1)} %get-tuple-element.40), channel_id=1, source_target_pairs={{0,6},{1,14},{2,0},{3,8},{4,2},{5,10},{6,4},{7,12},{8,7},{9,15},{1... | collective-permute-start | bytes 786440 | tf_op jit(solution)/shard_map/ppermute | solution.py:330
  97.7 4.5 %collective-permute-done.4.refs_2_ = bf16[2,128,512]{2,1,0:T(8,128)(2,1)S(1)} collective-permute-done((bf16[2,128,512]{2,1,0:T(8,128)(2,1)S(1)}, bf16[2,128,512]{2,1,0:T(8,128)(2,1)S(1)}, u32[]{:S(2)}, u32[]{:S(2)}) %collective-permute-start.4) | collective-permute-done | bytes 262176 | tf_op jit(solution)/shard_map/ppermute | solution.py:330
  102.3 7.7 %collective-permute-start.9 = (bf16[2,128,512]{2,1,0:T(8,128)(2,1)}, bf16[2,128,512]{2,1,0:T(8,128)(2,1)S(1)}, u32[]{:S(2)}, u32[]{:S(2)}) collective-permute-start(bf16[2,128,512]{2,1,0:T(8,128)(2,1)} %get-tuple-element.41), channel_id=1, source_target_pairs={{0,7},{1,15},{2,1},{3,9},{4,3},{5,11},{6,5},{7,13},{8,6},{9,14},{1... | collective-permute-start | bytes 786440 | tf_op jit(solution)/shard_map/ppermute | solution.py:330
  112.9 3.4 %collective-permute-done.9.refs_7_ = bf16[2,128,512]{2,1,0:T(8,128)(2,1)S(1)} collective-permute-done((bf16[2,128,512]{2,1,0:T(8,128)(2,1)}, bf16[2,128,512]{2,1,0:T(8,128)(2,1)S(1)}, u32[]{:S(2)}, u32[]{:S(2)}) %collective-permute-start.9) | collective-permute-done | bytes 262176 | tf_op jit(solution)/shard_map/ppermute | solution.py:330
  116.9 2.3 %collective-permute-done.10.other_ref = bf16[128,32,128]{2,1,0:T(8,128)(2,1)S(1)} collective-permute-done((bf16[128,32,128]{2,1,0:T(8,128)(2,1)S(1)}, bf16[128,32,128]{2,1,0:T(8,128)(2,1)S(1)}, u32[]{:S(2)}, u32[]{:S(2)}) %collective-permute-start.10) | collective-permute-done | bytes 1048608 | tf_op jit(solution)/shard_map/ppermute | solution.py:318
  119.2 4.1 %correlate.3 = (bf16[2,128,512]{2,1,0:T(8,128)(2,1)S(1)}, bf16[2,128,512]{2,1,0:T(8,128)(2,1)S(1)}, bf16[2,128,512]{2,1,0:T(8,128)(2,1)S(1)}, bf16[2,128,512]{2,...) custom-call(s32[2]{0:T(128)S(1)} %pad_add_fusion.2.at_ref, ...), custom_call_target="tpu_custom_call" | custom-call | flops 2147483648 | bytes 8388608 | tf_op jit(solution)/shard_map/correlate/pallas_call | solution.py:255
  124.5 4.0 %collective-permute-start.13 = (bf16[2,128,512]{2,1,0:T(8,128)(2,1)S(1)}, bf16[2,128,512]{2,1,0:T(8,128)(2,1)S(1)}, u32[]{:S(2)}, u32[]{:S(2)}) collective-permute-start(bf16[2,128,512]{2,1,0:T(8,128)(2,1)S(1)} %get-tuple-element.53), channel_id=1, source_target_pairs={{0,10},{1,2},{2,12},{3,4},{4,14},{5,6},{6,8},{7,0},{8,11},{9,3},{1... | collective-permute-start | bytes 786440 | tf_op jit(solution)/shard_map/ppermute | solution.py:330
  128.8 2.2 %collective-permute-start.15 = (bf16[2,128,512]{2,1,0:T(8,128)(2,1)}, bf16[2,128,512]{2,1,0:T(8,128)(2,1)S(1)}, u32[]{:S(2)}, u32[]{:S(2)}) collective-permute-start(bf16[2,128,512]{2,1,0:T(8,128)(2,1)} %get-tuple-element.55), channel_id=1, source_target_pairs={{0,12},{1,4},{2,14},{3,6},{4,8},{5,0},{6,10},{7,2},{8,13},{9,5},{1... | collective-permute-start | bytes 786440 | tf_op jit(solution)/shard_map/ppermute | solution.py:330
  131.5 5.6 %collective-permute-start.17 = (bf16[2,128,512]{2,1,0:T(8,128)(2,1)}, bf16[2,128,512]{2,1,0:T(8,128)(2,1)S(1)}, u32[]{:S(2)}, u32[]{:S(2)}) collective-permute-start(bf16[2,128,512]{2,1,0:T(8,128)(2,1)} %get-tuple-element.57), channel_id=1, source_target_pairs={{0,14},{1,6},{2,8},{3,0},{4,10},{5,2},{6,12},{7,4},{8,15},{9,7},{1... | collective-permute-start | bytes 786440 | tf_op jit(solution)/shard_map/ppermute | solution.py:330
  140.2 2.7 %widen.2.refs_0_ = f32[8,2,256,512]{3,2,1,0:T(8,128)} custom-call(s32[2,8]{1,0:T(2,128)S(1)} %get-tuple-element.59.where_ref, bf16[2,128,512]{2,1,0:T(8,128)(2,1)S(1)} %collective-permute-done.2.refs_0_, bf16[2,128,512]{2,1,0:T(8,128)(2,1)S(1)} %collective-permute-done.3.refs_1_, bf16[2,128,512]{2,1,0:T(8,128)(2,1)S(1)} %collective-permute-done.4.refs_2_, ...), custom_call_target="tpu_custom_call" | custom-call | flops 1048576 | bytes 6291456 | tf_op jit(solution)/shard_map/widen/pallas_call | solution.py:284
  142.8 6.1 %collective-permute-done.14.refs_4_ = bf16[2,128,512]{2,1,0:T(8,128)(2,1)S(1)} collective-permute-done((bf16[2,128,512]{2,1,0:T(8,128)(2,1)}, bf16[2,128,512]{2,1,0:T(8,128)(2,1)S(1)}, u32[]{:S(2)}, u32[]{:S(2)}) %collective-permute-start.14) | collective-permute-done | bytes 262176 | tf_op jit(solution)/shard_map/ppermute | solution.py:330
  150.7 2.5 %collective-permute-done.16.refs_6_ = bf16[2,128,512]{2,1,0:T(8,128)(2,1)S(1)} collective-permute-done((bf16[2,128,512]{2,1,0:T(8,128)(2,1)}, bf16[2,128,512]{2,1,0:T(8,128)(2,1)S(1)}, u32[]{:S(2)}, u32[]{:S(2)}) %collective-permute-start.16) | collective-permute-done | bytes 262176 | tf_op jit(solution)/shard_map/ppermute | solution.py:330
  153.2 2.7 %collective-permute-done.17.refs_7_ = bf16[2,128,512]{2,1,0:T(8,128)(2,1)S(1)} collective-permute-done((bf16[2,128,512]{2,1,0:T(8,128)(2,1)}, bf16[2,128,512]{2,1,0:T(8,128)(2,1)S(1)}, u32[]{:S(2)}, u32[]{:S(2)}) %collective-permute-start.17) | collective-permute-done | bytes 262176 | tf_op jit(solution)/shard_map/ppermute | solution.py:330
  155.9 2.7 %widen.3 = f32[8,2,256,512]{3,2,1,0:T(8,128)} custom-call(s32[2,8]{1,0:T(2,128)S(1)} %get-tuple-element.60.where_ref, f32[8,2,256,512]{3,2,1,0:T(8,128)} %widen.2.refs_0_, bf16[2,128,512]{2,1,0:T(8,128)(2,1)S(1)} %collective-permute-done.11.refs_1_, bf16[2,128,512]{2,1,0:T(8,128)(2,1)S(1)} %collective-permute-done.12.refs_2_, ...), custom_call_target="tpu_custom_call", output_to_operand_aliasing={{}: (1, {})} | custom-call | flops 1048576 | bytes 6291456 | tf_op jit(solution)/shard_map/widen/pallas_call | solution.py:284
  (56 shorter events, 30.2 us)
Async XLA Ops:
  0.0 33.9 %copy-start.10 = (bf16[256,512]{1,0:T(8,128)(2,1)S(1)}, bf16[256,512]{1,0:T(8,128)(2,1)}, u32[]{:S(2)}) copy-start(bf16[256,512]{1,0:T(8,128)(2,1)} %constant.79.clone.tab_ref) | copy-start | bytes 786436
  1.0 9.3 %collective-permute-start = (bf16[32,3584]{1,0:T(8,128)(2,1)S(1)}, bf16[32,3584]{1,0:T(8,128)(2,1)S(1)}, u32[]{:S(2)}, u32[]{:S(2)}) collective-permute-start(bf16[32,3584]{1,0:T(8,128)(2,1)S(1)} %slice.7), channel_id=1, source_target_pairs={{0,1},{1,2},{2,3},{3,4},{4,5},{5,6},{6,7},{8,9},{9,10},{10,11},{11... | collective-permute-start | bytes 688136 | tf_op jit(solution)/shard_map/ppermute | solution.py:304
  17.6 42.5 %all-to-all-start.1 = ((bf16[128,32,128]{2,1,0:T(8,128)(2,1)}), bf16[128,32,128]{2,1,0:T(8,128)(2,1)S(1)}, u32[]{:S(2)}, u32[]{:S(2)}) async-start(bf16[128,32,128]{2,1,0:T(8,128)(2,1)} %get-tuple-element.33), calls=%async_computation.1 | async-start | bytes 2097152 | tf_op jit(solution)/shard_map/all_to_all | solution.py:312
  60.1 49.9 %all-to-all-start = ((bf16[128,32,128]{2,1,0:T(8,128)(2,1)}), bf16[128,32,128]{2,1,0:T(8,128)(2,1)S(1)}, u32[]{:S(2)}, u32[]{:S(2)}) async-start(bf16[128,32,128]{2,1,0:T(8,128)(2,1)} %dft.1), calls=%async_computation | async-start | bytes 2097152 | tf_op jit(solution)/shard_map/all_to_all | solution.py:312
  70.0 4.7 %collective-permute-start.1 = (bf16[128,32,128]{2,1,0:T(8,128)(2,1)S(1)}, bf16[128,32,128]{2,1,0:T(8,128)(2,1)S(1)}, u32[]{:S(2)}, u32[]{:S(2)}) collective-permute-start(bf16[128,32,128]{2,1,0:T(8,128)(2,1)S(1)} %all-to-all-done.1.mine_ref), channel_id=1, source_target_pairs={{0,8},{8,0},{1,9},{9,1},{2,10},{10,2},{3,11},{11,3},{4,12},{12,4},... | collective-permute-start | bytes 3145736 | tf_op jit(solution)/shard_map/ppermute | solution.py:318
  78.8 14.4 %collective-permute-start.2 = (bf16[2,128,512]{2,1,0:T(8,128)(2,1)S(1)}, bf16[2,128,512]{2,1,0:T(8,128)(2,1)S(1)}, u32[]{:S(2)}, u32[]{:S(2)}) collective-permute-start(bf16[2,128,512]{2,1,0:T(8,128)(2,1)S(1)} %get-tuple-element.34), channel_id=1, source_target_pairs={{0,0},{1,8},{2,2},{3,10},{4,4},{5,12},{6,6},{7,14},{8,1},{9,9},{10... | collective-permute-start | bytes 786440 | tf_op jit(solution)/shard_map/ppermute | solution.py:330
  81.9 12.5 %collective-permute-start.3 = (bf16[2,128,512]{2,1,0:T(8,128)(2,1)S(1)}, bf16[2,128,512]{2,1,0:T(8,128)(2,1)S(1)}, u32[]{:S(2)}, u32[]{:S(2)}) collective-permute-start(bf16[2,128,512]{2,1,0:T(8,128)(2,1)S(1)} %get-tuple-element.35), channel_id=1, source_target_pairs={{0,1},{1,9},{2,3},{3,11},{4,5},{5,13},{6,7},{7,15},{8,0},{9,8},{10... | collective-permute-start | bytes 786440 | tf_op jit(solution)/shard_map/ppermute | solution.py:330
  82.0 20.3 %collective-permute-start.4 = (bf16[2,128,512]{2,1,0:T(8,128)(2,1)S(1)}, bf16[2,128,512]{2,1,0:T(8,128)(2,1)S(1)}, u32[]{:S(2)}, u32[]{:S(2)}) collective-permute-start(bf16[2,128,512]{2,1,0:T(8,128)(2,1)S(1)} %get-tuple-element.36), channel_id=1, source_target_pairs={{0,2},{1,10},{2,4},{3,12},{4,6},{5,14},{6,0},{7,8},{8,3},{9,11},{1... | collective-permute-start | bytes 786440 | tf_op jit(solution)/shard_map/ppermute | solution.py:330
  83.2 26.7 %collective-permute-start.5 = (bf16[2,128,512]{2,1,0:T(8,128)(2,1)}, bf16[2,128,512]{2,1,0:T(8,128)(2,1)S(1)}, u32[]{:S(2)}, u32[]{:S(2)}) collective-permute-start(bf16[2,128,512]{2,1,0:T(8,128)(2,1)} %get-tuple-element.37), channel_id=1, source_target_pairs={{0,3},{1,11},{2,5},{3,13},{4,7},{5,15},{6,1},{7,9},{8,2},{9,10},{1... | collective-permute-start | bytes 786440 | tf_op jit(solution)/shard_map/ppermute | solution.py:330
  85.2 24.8 %collective-permute-start.6 = (bf16[2,128,512]{2,1,0:T(8,128)(2,1)}, bf16[2,128,512]{2,1,0:T(8,128)(2,1)S(1)}, u32[]{:S(2)}, u32[]{:S(2)}) collective-permute-start(bf16[2,128,512]{2,1,0:T(8,128)(2,1)} %get-tuple-element.38), channel_id=1, source_target_pairs={{0,4},{1,12},{2,6},{3,14},{4,0},{5,8},{6,2},{7,10},{8,5},{9,13},{1... | collective-permute-start | bytes 786440 | tf_op jit(solution)/shard_map/ppermute | solution.py:330
  93.3 18.8 %collective-permute-start.7 = (bf16[2,128,512]{2,1,0:T(8,128)(2,1)}, bf16[2,128,512]{2,1,0:T(8,128)(2,1)S(1)}, u32[]{:S(2)}, u32[]{:S(2)}) collective-permute-start(bf16[2,128,512]{2,1,0:T(8,128)(2,1)} %get-tuple-element.39), channel_id=1, source_target_pairs={{0,5},{1,13},{2,7},{3,15},{4,1},{5,9},{6,3},{7,11},{8,4},{9,12},{1... | collective-permute-start | bytes 786440 | tf_op jit(solution)/shard_map/ppermute | solution.py:330
  94.4 18.5 %collective-permute-start.8 = (bf16[2,128,512]{2,1,0:T(8,128)(2,1)}, bf16[2,128,512]{2,1,0:T(8,128)(2,1)S(1)}, u32[]{:S(2)}, u32[]{:S(2)}) collective-permute-start(bf16[2,128,512]{2,1,0:T(8,128)(2,1)} %get-tuple-element.40), channel_id=1, source_target_pairs={{0,6},{1,14},{2,0},{3,8},{4,2},{5,10},{6,4},{7,12},{8,7},{9,15},{1... | collective-permute-start | bytes 786440 | tf_op jit(solution)/shard_map/ppermute | solution.py:330
  102.3 14.1 %collective-permute-start.9 = (bf16[2,128,512]{2,1,0:T(8,128)(2,1)}, bf16[2,128,512]{2,1,0:T(8,128)(2,1)S(1)}, u32[]{:S(2)}, u32[]{:S(2)}) collective-permute-start(bf16[2,128,512]{2,1,0:T(8,128)(2,1)} %get-tuple-element.41), channel_id=1, source_target_pairs={{0,7},{1,15},{2,1},{3,9},{4,3},{5,11},{6,5},{7,13},{8,6},{9,14},{1... | collective-permute-start | bytes 786440 | tf_op jit(solution)/shard_map/ppermute | solution.py:330
  112.1 16.7 %copy-start.3 = (bf16[2,128,512]{2,1,0:T(8,128)(2,1)}, bf16[2,128,512]{2,1,0:T(8,128)(2,1)S(1)}, u32[]{:S(2)}) copy-start(bf16[2,128,512]{2,1,0:T(8,128)(2,1)S(1)} %collective-permute-done.7.refs_5_) | copy-start | bytes 786436
  112.9 18.1 %copy-start.5 = (bf16[2,128,512]{2,1,0:T(8,128)(2,1)}, bf16[2,128,512]{2,1,0:T(8,128)(2,1)S(1)}, u32[]{:S(2)}) copy-start(bf16[2,128,512]{2,1,0:T(8,128)(2,1)S(1)} %collective-permute-done.8.refs_6_) | copy-start | bytes 786436
  116.3 2.8 %collective-permute-start.10 = (bf16[128,32,128]{2,1,0:T(8,128)(2,1)S(1)}, bf16[128,32,128]{2,1,0:T(8,128)(2,1)S(1)}, u32[]{:S(2)}, u32[]{:S(2)}) collective-permute-start(bf16[128,32,128]{2,1,0:T(8,128)(2,1)S(1)} %all-to-all-done.mine_ref), channel_id=1, source_target_pairs={{0,8},{8,0},{1,9},{9,1},{2,10},{10,2},{3,11},{11,3},{4,12},{12,4},... | collective-permute-start | bytes 3145736 | tf_op jit(solution)/shard_map/ppermute | solution.py:318
  123.3 7.7 %collective-permute-start.11 = (bf16[2,128,512]{2,1,0:T(8,128)(2,1)S(1)}, bf16[2,128,512]{2,1,0:T(8,128)(2,1)S(1)}, u32[]{:S(2)}, u32[]{:S(2)}) collective-permute-start(bf16[2,128,512]{2,1,0:T(8,128)(2,1)S(1)} %get-tuple-element.51), channel_id=1, source_target_pairs={{0,8},{1,0},{2,10},{3,2},{4,12},{5,4},{6,14},{7,6},{8,9},{9,1},{10... | collective-permute-start | bytes 786440 | tf_op jit(solution)/shard_map/ppermute | solution.py:330
  123.9 7.6 %collective-permute-start.12 = (bf16[2,128,512]{2,1,0:T(8,128)(2,1)S(1)}, bf16[2,128,512]{2,1,0:T(8,128)(2,1)S(1)}, u32[]{:S(2)}, u32[]{:S(2)}) collective-permute-start(bf16[2,128,512]{2,1,0:T(8,128)(2,1)S(1)} %get-tuple-element.52), channel_id=1, source_target_pairs={{0,9},{1,1},{2,11},{3,3},{4,13},{5,5},{6,15},{7,7},{8,8},{9,0},{10... | collective-permute-start | bytes 786440 | tf_op jit(solution)/shard_map/ppermute | solution.py:330
  124.5 12.5 %collective-permute-start.13 = (bf16[2,128,512]{2,1,0:T(8,128)(2,1)S(1)}, bf16[2,128,512]{2,1,0:T(8,128)(2,1)S(1)}, u32[]{:S(2)}, u32[]{:S(2)}) collective-permute-start(bf16[2,128,512]{2,1,0:T(8,128)(2,1)S(1)} %get-tuple-element.53), channel_id=1, source_target_pairs={{0,10},{1,2},{2,12},{3,4},{4,14},{5,6},{6,8},{7,0},{8,11},{9,3},{1... | collective-permute-start | bytes 786440 | tf_op jit(solution)/shard_map/ppermute | solution.py:330
  128.5 20.4 %collective-permute-start.14 = (bf16[2,128,512]{2,1,0:T(8,128)(2,1)}, bf16[2,128,512]{2,1,0:T(8,128)(2,1)S(1)}, u32[]{:S(2)}, u32[]{:S(2)}) collective-permute-start(bf16[2,128,512]{2,1,0:T(8,128)(2,1)} %get-tuple-element.54), channel_id=1, source_target_pairs={{0,11},{1,3},{2,13},{3,5},{4,15},{5,7},{6,9},{7,1},{8,10},{9,2},{1... | collective-permute-start | bytes 786440 | tf_op jit(solution)/shard_map/ppermute | solution.py:330
  128.8 21.9 %collective-permute-start.15 = (bf16[2,128,512]{2,1,0:T(8,128)(2,1)}, bf16[2,128,512]{2,1,0:T(8,128)(2,1)S(1)}, u32[]{:S(2)}, u32[]{:S(2)}) collective-permute-start(bf16[2,128,512]{2,1,0:T(8,128)(2,1)} %get-tuple-element.55), channel_id=1, source_target_pairs={{0,12},{1,4},{2,14},{3,6},{4,8},{5,0},{6,10},{7,2},{8,13},{9,5},{1... | collective-permute-start | bytes 786440 | tf_op jit(solution)/shard_map/ppermute | solution.py:330
  131.0 22.2 %collective-permute-start.16 = (bf16[2,128,512]{2,1,0:T(8,128)(2,1)}, bf16[2,128,512]{2,1,0:T(8,128)(2,1)S(1)}, u32[]{:S(2)}, u32[]{:S(2)}) collective-permute-start(bf16[2,128,512]{2,1,0:T(8,128)(2,1)} %get-tuple-element.56), channel_id=1, source_target_pairs={{0,13},{1,5},{2,15},{3,7},{4,9},{5,1},{6,11},{7,3},{8,12},{9,4},{1... | collective-permute-start | bytes 786440 | tf_op jit(solution)/shard_map/ppermute | solution.py:330
  131.5 24.4 %collective-permute-start.17 = (bf16[2,128,512]{2,1,0:T(8,128)(2,1)}, bf16[2,128,512]{2,1,0:T(8,128)(2,1)S(1)}, u32[]{:S(2)}, u32[]{:S(2)}) collective-permute-start(bf16[2,128,512]{2,1,0:T(8,128)(2,1)} %get-tuple-element.57), channel_id=1, source_target_pairs={{0,14},{1,6},{2,8},{3,0},{4,10},{5,2},{6,12},{7,4},{8,15},{9,7},{1... | collective-permute-start | bytes 786440 | tf_op jit(solution)/shard_map/ppermute | solution.py:330
  137.0 18.9 %collective-permute-start.18 = (bf16[2,128,512]{2,1,0:T(8,128)(2,1)}, bf16[2,128,512]{2,1,0:T(8,128)(2,1)S(1)}, u32[]{:S(2)}, u32[]{:S(2)}) collective-permute-start(bf16[2,128,512]{2,1,0:T(8,128)(2,1)} %get-tuple-element.58), channel_id=1, source_target_pairs={{0,15},{1,7},{2,9},{3,1},{4,11},{5,3},{6,13},{7,5},{8,14},{9,6},{1... | collective-permute-start | bytes 786440 | tf_op jit(solution)/shard_map/ppermute | solution.py:330
  (9 other events, 25.1 us)

commit v4 on v3

v4 whole, which is shorter than its diff:
```python
import functools

import jax
import jax.numpy as jnp
import ml_dtypes
import numpy as np
from jax import lax
from jax.experimental import pallas as pl
from jax.experimental.pallas import tpu as pltpu
from jax.sharding import PartitionSpec as P

FFT_LEN = 512
TAPS = 8
CHANNELS = 256
LANES = 128
HEAD = 8
CHUNKS = FFT_LEN // LANES
ALL = ("chan", "row", "col")
VMEM = pl.BlockSpec(memory_space=pltpu.VMEM)
SMEM = pl.BlockSpec(memory_space=pltpu.SMEM)
NT = (((1,), (1,)), ((), ()))


def window_table(taps, length):
    count = taps * length
    position = np.arange(count, dtype=np.float64)
    offset = (position - count / 2 + 0.5) / length
    taper = 0.5 - 0.5 * np.cos(2.0 * np.pi * (position + 0.5) / count)
    values = np.sinc(offset) * taper
    values = values / np.sqrt(np.sum(values * values))
    return values.reshape(taps, length).astype(np.float32)


def fourier_table(channels, length):
    channel_index = np.arange(channels)[:, None]
    sample_index = np.arange(length)[None, :]
    phase = (channel_index * sample_index % length) * (2.0 * np.pi / length)
    return np.stack([np.cos(phase), -np.sin(phase)]).astype(np.float32).astype(ml_dtypes.bfloat16)


def fir_rows(read, first, last, store, w_ref, rows, lane):
    height = rows.size
    taps = [jnp.broadcast_to(w_ref[t : t + 1, pl.ds(lane, LANES)], (height, LANES)) for t in range(TAPS)]
    sums = {}
    for block in range(first, last + TAPS - 1):
        value = read(block).astype(jnp.float32)
        for t in range(TAPS):
            s = block - t
            if first <= s < last:
                term = taps[t] * value
                sums[s] = term if t == 0 else sums[s] + term
        done = block - TAPS + 1
        if done >= first:
            store(done, sums.pop(done))


def for_tiles(inputs, body):
    row_tile = 16

    def step(index, carry):
        chunk = index % CHUNKS
        first_row = pl.multiple_of((index // CHUNKS) * row_tile, row_tile)
        body(pl.ds(first_row, row_tile), first_row, chunk, pl.multiple_of(chunk * LANES, LANES))
        return carry

    lax.fori_loop(0, (inputs // row_tile) * CHUNKS, step, 0)


def fir_kernel(v_ref, w_ref, f_ref):
    inputs = v_ref.shape[0]
    spectra = v_ref.shape[1] // FFT_LEN
    body_len = spectra - HEAD

    def tile(rows, first_row, chunk, lane):
        def read(block):
            return v_ref[rows, pl.ds((block - TAPS + 1) * FFT_LEN + lane, LANES)]

        def store(s, value):
            f_ref[chunk, pl.ds(first_row * body_len + s - HEAD, rows.size, stride=body_len), :] = value

        fir_rows(read, HEAD, spectra, store, w_ref, rows, lane)

    for_tiles(inputs, tile)


def dft(f_ref, head_ref, tab_ref, o_ref, t_ref):
    inputs = o_ref.shape[1]
    channels = tab_ref.shape[0] // 2
    body_len = f_ref.shape[1] // inputs
    spectra = body_len + HEAD
    group = 8
    low = lax.broadcasted_iota(jnp.int32, (channels, LANES), 1) < spectra

    def transform(step, carry):
        columns = []
        for c in range(CHUNKS):
            parts = []
            for j in range(group):
                i = step * group + j
                parts.append(head_ref[c, pl.ds(pl.multiple_of(i * HEAD, HEAD), HEAD), :])
                parts.append(f_ref[c, pl.ds(pl.multiple_of(i * body_len, 8), body_len), :])
            columns.append(jnp.concatenate(parts, axis=0).astype(jnp.bfloat16))
        block = jnp.concatenate(columns, axis=1)
        both = lax.dot_general(tab_ref[...], block, NT, preferred_element_type=jnp.float32)
        for pair in range(group // 2):
            cut = slice(pair * LANES, (pair + 1) * LANES)
            re, im = both[:channels, cut], both[channels:, cut]
            even = jnp.where(low, re, pltpu.roll(im, spectra, 1))
            odd = jnp.where(low, pltpu.roll(re, spectra, 1), im)
            row = step * group + 2 * pair
            t_ref[pl.ds(row, channels, stride=inputs), :] = even
            t_ref[pl.ds(row + 1, channels, stride=inputs), :] = odd
        return carry

    lax.fori_loop(0, inputs // group, transform, 0)

    step = 8

    def cast(index, carry):
        for j in range(step):
            first = pl.multiple_of((index * step + j) * inputs, inputs)
            o_ref[index * step + j] = t_ref[pl.ds(first, inputs), :].astype(jnp.bfloat16)
        return carry

    lax.fori_loop(0, channels // step, cast, 0)


def head_kernel(v_ref, h_ref, f_ref, w_ref, tab_ref, o_ref, head_ref, t_ref):
    def tile(rows, first_row, chunk, lane):
        def read(block):
            if block < TAPS - 1:
                return h_ref[rows, pl.ds(block * FFT_LEN + lane, LANES)]
            return v_ref[rows, pl.ds((block - TAPS + 1) * FFT_LEN + lane, LANES)]

        def store(s, value):
            head_ref[chunk, pl.ds(first_row * HEAD + s, rows.size, stride=HEAD), :] = value

        fir_rows(read, 0, HEAD, store, w_ref, rows, lane)

    for_tiles(v_ref.shape[0], tile)
    dft(f_ref, head_ref, tab_ref, o_ref, t_ref)


def params(mib=12):
    return pltpu.CompilerParams(vmem_limit_bytes=mib << 20)


def cost(flops, nbytes):
    return pl.CostEstimate(flops=flops, bytes_accessed=nbytes, transcendentals=0)


def channelize(voltages, earlier):
    inputs = voltages.shape[0]
    spectra = voltages.shape[1] // FFT_LEN
    window = window_table(TAPS, FFT_LEN)
    table = fourier_table(CHANNELS, FFT_LEN).reshape(-1, FFT_LEN)
    body = pl.pallas_call(
        fir_kernel,
        out_shape=jax.ShapeDtypeStruct((CHUNKS, inputs * (spectra - HEAD), LANES), jnp.float32),
        in_specs=[VMEM] * 2,
        out_specs=VMEM,
        compiler_params=params(),
        cost_estimate=cost(16 * voltages.size, 6 * voltages.size),
        name="fir",
    )(voltages, window)
    return pl.pallas_call(
        head_kernel,
        out_shape=jax.ShapeDtypeStruct((CHANNELS, inputs, 2 * spectra), jnp.bfloat16),
        in_specs=[VMEM] * 5,
        out_specs=VMEM,
        scratch_shapes=[
            pltpu.VMEM((CHUNKS, inputs * HEAD, LANES), jnp.float32),
            pltpu.VMEM((CHANNELS * inputs, 2 * spectra), jnp.float32),
        ],
        compiler_params=params(),
        cost_estimate=cost(4 * CHANNELS * FFT_LEN * inputs * spectra, 6 * voltages.size),
        name="head_dft",
    )(voltages[:, : HEAD * FFT_LEN], earlier, body, window, table)


def correlate_kernel(groups, rows, cols, shifts, scale, at_ref, got_ref, *refs):
    outs, (x_ref, l_ref) = refs[:-2], refs[-2:]
    row, col = at_ref[0], at_ref[1]
    height = got_ref.shape[1]
    slots = rows * cols
    half = LANES // 2

    def place(g, carry):
        dest = pl.ds(pl.multiple_of(g * height, height), height)
        for t in range(slots):
            x_ref[dest, t * LANES : (t + 1) * LANES] = got_ref[g * slots + t]
        return carry

    lax.fori_loop(0, groups, place, 0)

    row_block = x_ref.shape[0] // rows
    col_block = x_ref.shape[0] // cols
    upper = lax.broadcasted_iota(jnp.int32, (row_block, LANES), 1) >= half
    for n, dy in enumerate(shifts):
        first = pl.multiple_of(lax.rem(row + dy, rows) * row_block, row_block)
        for t in range(slots):
            lanes = slice(t * LANES, (t + 1) * LANES)
            value = x_ref[pl.ds(first, row_block), lanes]
            turned = pltpu.roll(value.astype(jnp.float32), half, 1)
            l_ref[:row_block, lanes] = value
            l_ref[row_block:, lanes] = jnp.where(upper, -turned, turned).astype(jnp.bfloat16)
        for d in range(cols):
            block = pl.multiple_of(lax.rem(col + d, cols) * col_block, col_block)
            right = x_ref[pl.ds(block, col_block), :]
            value = lax.dot_general(l_ref[...], right, NT, preferred_element_type=jnp.float32) * scale
            for p in range(2):
                outs[n * cols + d][p] = value[p * row_block : (p + 1) * row_block].astype(jnp.bfloat16)


def correlate(at, got, groups, rows, cols, shifts, scale):
    total = groups * got.shape[1]
    depth = rows * cols * LANES
    row_block, col_block = total // rows, total // cols
    piece = jax.ShapeDtypeStruct((2, row_block, col_block), jnp.bfloat16)
    count = len(shifts) * cols
    return pl.pallas_call(
        functools.partial(correlate_kernel, groups, rows, cols, shifts, scale),
        out_shape=[piece] * count,
        in_specs=[SMEM, VMEM],
        out_specs=[VMEM] * count,
        scratch_shapes=[pltpu.VMEM((total, depth), jnp.bfloat16), pltpu.VMEM((2 * row_block, depth), jnp.bfloat16)],
        compiler_params=params(),
        cost_estimate=cost(4 * count * row_block * col_block * depth, 2 * total * depth + 2 * count * piece.size),
        name="correlate",
    )(at, got)


def widen_kernel(count, where_ref, *refs):
    pieces, o_ref, wide_ref, sems = refs[-count - 3 : -3], refs[-3], refs[-2], refs[-1]
    copies = []
    for j, piece in enumerate(pieces):
        wide_ref[j] = piece[...].astype(jnp.float32)
        copies.append(pltpu.make_async_copy(wide_ref.at[j], o_ref.at[where_ref[j]], sems.at[j]))
        copies[-1].start()
    for copy in copies:
        copy.wait()


def widen(pieces, where, shape, into=None):
    count, piece = len(pieces), pieces[0]
    before = [] if into is None else [into]
    anywhere = pl.BlockSpec(memory_space=pl.ANY)
    return pl.pallas_call(
        functools.partial(widen_kernel, count),
        in_specs=[SMEM] + [anywhere] * len(before) + [VMEM] * count,
        out_specs=anywhere,
        out_shape=jax.ShapeDtypeStruct(shape, jnp.float32),
        scratch_shapes=[pltpu.VMEM((count, *piece.shape), jnp.float32), pltpu.SemaphoreType.DMA((count,))],
        input_output_aliases={1: 0} if before else {},
        compiler_params=params(8),
        cost_estimate=cost(count * piece.size, 6 * count * piece.size),
        name="widen",
    )(where, *before, *pieces)


def per_device(voltages):
    slot_spectra = voltages.shape[1] // FFT_LEN
    rows = lax.axis_size("row")
    cols = lax.axis_size("col")
    slots = rows * cols
    groups = lax.axis_size("chan")
    tail = voltages[:, (slot_spectra - TAPS + 1) * FFT_LEN :]
    earlier = lax.ppermute(tail, ("row", "col"), [(i, i + 1) for i in range(slots - 1)])
    row, col = lax.axis_index("row"), lax.axis_index("col")
    at = jnp.stack([row, col]).astype(jnp.int32)
    scale = 1.0 / (slot_spectra * slots)
    total = groups * voltages.shape[0]
    shape = (slots, 2, total // rows, total // cols)
    message = channelize(voltages, earlier)
    turned = lax.all_to_all(message, ALL, split_axis=0, concat_axis=0, tiled=True)

    def travel(piece, dy, d):
        links = [(r * cols + c, (r + dy) % rows * cols + (c + d) % cols) for r in range(rows) for c in range(cols)]
        return piece if dy == d == 0 else lax.ppermute(piece, ("row", "col"), links)

    arrived = []
    for shifts in ((2,), (1, 3), (0,)):
        sent = correlate(at, turned, groups, rows, cols, shifts, scale)
        turned, sent = lax.optimization_barrier((turned, sent))
        for n, dy in enumerate(shifts):
            for d in range(cols):
                channel = (row + rows - dy) % rows * cols + (col + cols - d) % cols
                arrived.append((travel(sent[n * cols + d], dy, d), channel))
    out = None
    for batch in ((6, 0, 1), (2, 3), (4, 5, 7)):
        where = jnp.stack([arrived[b][1] for b in batch]).astype(jnp.int32)
        out = widen([arrived[b][0] for b in batch], where, shape, out)
    return out


def solution(mesh):
    return jax.shard_map(
        per_device,
        mesh=mesh,
        in_specs=(P("chan", ("row", "col")),),
        out_specs=P("chan", None, "row", "col"),
        check_vma=False,
    )
```

time: 159 us -> 157 us (0.987)
  starting transfers between devices: 66.3 us -> 27.7 us
  waiting for transfers between devices: 55.6 us -> 93.3 us
  local copies, waits for them, and re-layouts: 12.2 us -> 7.96 us
  Pallas kernels: 24.2 us -> 26.6 us
    all_to_all x2 -> x1, waiting for transfers between devices: 20 us -> 54.9 us  [per_device(): lax.all_to_all(message, ALL, split_axis=0, concat_axis=0, tiled=True)]
    ppermute x18 -> x7, starting transfers between devices: 36.1 us -> 7.22 us  [travel(): return piece if dy == d == 0 else lax.ppermute(piece, ('row', 'col'), links)]
    all_to_all x2 -> x1, starting transfers between devices: 26.2 us -> 16.5 us  [per_device(): lax.all_to_all(message, ALL, split_axis=0, concat_axis=0, tiled=True)]
    unnamed x24 -> x14, local copies, waits for them, and re-layouts: 9.98 us -> 5.98 us
    ppermute x18 -> x7, waiting for transfers between devices: 35.6 us -> 38.4 us  [travel(): return piece if dy == d == 0 else lax.ppermute(piece, ('row', 'col'), links)]
    pallas_call x2 -> x3, Pallas kernels: 5.3 us -> 7.55 us  [widen(): pl.pallas_call(functools.partial(widen_kernel, count), in_specs=[SMEM] +...]
  transfers between devices with their start and end apart: 21 -> 9, of which waited for: 13 -> 5; matrix products, arithmetic and copies ran while one was open for 1% -> 1% of each run, Pallas kernels for 8% -> 9%
where the time goes in v4:
time: 157 us; the launch traced here: 156 us
  waiting for transfers between devices  93.3 us (59%)
  starting transfers between devices  27.7 us (18%)
  Pallas kernels  26.6 us (17%)
  local copies, waits for them, and re-layouts  7.96 us (5%)
    all_to_all x1, waiting for transfers between devices, per_device(): lax.all_to_all(message, ALL, split_axis=0, concat_axis=0, tiled=True)  54.9 us
    ppermute x7, waiting for transfers between devices, travel(): return piece if dy == d == 0 else lax.ppermute(piece, ('row', 'col'), links)  38.4 us
    all_to_all x1, starting transfers between devices, per_device(): lax.all_to_all(message, ALL, split_axis=0, concat_axis=0, tiled=True)  16.5 us
    pallas_call x3, Pallas kernels, correlate(): pl.pallas_call(functools.partial(correlate_kernel, groups, rows, cols, sh...  9.76 us
    pallas_call x3, Pallas kernels, widen(): pl.pallas_call(functools.partial(widen_kernel, count), in_specs=[SMEM] +...  7.55 us
    pallas_call x1, Pallas kernels, channelize(): pl.pallas_call(head_kernel, out_shape=jax.ShapeDtypeStruct((CHANNELS, inp...  7.24 us
    ppermute x7, starting transfers between devices, travel(): return piece if dy == d == 0 else lax.ppermute(piece, ('row', 'col'), links)  7.22 us
    unnamed x14, local copies, waits for them, and re-layouts  5.98 us
  transfers between devices with their start and end apart: 9, of which 5 were waited for; matrix products, arithmetic and copies ran while one was open for 1% of the time, Pallas kernels for 9%

profile of v4, /device:TPU:1, one launch (start us, length us, event | category | flops | bytes accessed | tf_op | source)
XLA Modules:
  0.0 155.9 jit_solution(13659986130424721673)
XLA Ops:
  0.0 1.0 slice.7
  1.0 4.0 %collective-permute-start = (bf16[32,3584]{1,0:T(8,128)(2,1)S(1)}, bf16[32,3584]{1,0:T(8,128)(2,1)S(1)}, u32[]{:S(2)}, u32[]{:S(2)}) collective-permute-start(bf16[32,3584]{1,0:T(8,128)(2,1)S(1)} %slice.7), channel_id=1, source_target_pairs={{0,1},{1,2},{2,3},{3,4},{4,5},{5,6},{6,7},{8,9},{9,10},{10,11},{11... | collective-permute-start | bytes 688136 | tf_op jit(solution)/shard_map/ppermute | solution.py:268
  5.0 1.0 slice.6.v_ref
  6.0 1.6 %copy-done = bf16[32,32768]{1,0:T(8,128)(2,1)S(1)} copy-done((bf16[32,32768]{1,0:T(8,128)(2,1)S(1)}, bf16[32,32768]{1,0:T(8,128)(2,1)}, u32[]{:S(2)}) %copy-start) | copy-done | bytes 2097176
  8.3 2.0 %fir.1.f_ref = f32[4,1792,128]{2,1,0:T(8,128)S(1)} custom-call(bf16[32,32768]{1,0:T(8,128)(2,1)S(1)} %copy-done, f32[8,512]{1,0:T(8,128)S(1)} %copy-done.6), custom_call_target="tpu_custom_call" | custom-call | flops 16777216 | bytes 6291456 | tf_op jit(solution)/shard_map/fir/pallas_call | solution.py:157
  10.3 7.2 %head_dft.1 = bf16[256,32,128]{2,1,0:T(8,128)(2,1)} custom-call(bf16[32,4096]{1,0:T(8,128)(2,1)S(1)} %slice.6.v_ref, bf16[32,3584]{1,0:T(8,128)(2,1)S(1)} %collective-permute-done.h_ref, f32[4,1792,128]{2,1,0:T(8,128)S(1)} %fir.1.f_ref, f32[8,512]{1,0:T(8,128)S(1)} %copy-done.6, bf16[512,512]{1,0:T(8,128)(2,1)S(1)} %copy-done.5), custom_call_target="tpu_custom_call" | custom-call | flops 1073741824 | bytes 6291456 | tf_op jit(solution)/shard_map/head_dft/pallas_call | solution.py:166
  17.6 16.5 %all-to-all-start = ((bf16[256,32,128]{2,1,0:T(8,128)(2,1)}), bf16[256,32,128]{2,1,0:T(8,128)(2,1)S(1)}, u32[]{:S(2)}, u32[]{:S(2)}) async-start(bf16[256,32,128]{2,1,0:T(8,128)(2,1)} %head_dft.1), calls=%async_computation | async-start | bytes 4194304 | tf_op jit(solution)/shard_map/all_to_all | solution.py:275
  34.1 54.9 %all-to-all-done.got_ref = bf16[256,32,128]{2,1,0:T(8,128)(2,1)S(1)} async-done(((bf16[256,32,128]{2,1,0:T(8,128)(2,1)}), bf16[256,32,128]{2,1,0:T(8,128)(2,1)S(1)}, u32[]{:S(2)}, u32[]{:S(2)}) %all-to-all-start) | async-done | bytes 2097184 | tf_op jit(solution)/shard_map/all_to_all | solution.py:275
  89.0 2.4 %correlate.3 = (bf16[2,256,512]{2,1,0:T(8,128)(2,1)S(1)}, bf16[2,256,512]{2,1,0:T(8,128)(2,1)S(1)}) custom-call(s32[2]{0:T(128)S(1)} %pad_add_fusion.3.at_ref, bf16[256,32,128]{2,1,0:T(8,128)(2,1)S(1)} %all-to-all-done.got_ref), custom_call_target="tpu_custom_call" | custom-call | flops 1073741824 | bytes 3145728 | tf_op jit(solution)/shard_map/correlate/pallas_call | solution.py:221
  91.5 3.0 %collective-permute-start.2 = (bf16[2,256,512]{2,1,0:T(8,128)(2,1)S(1)}, bf16[2,256,512]{2,1,0:T(8,128)(2,1)S(1)}, u32[]{:S(2)}, u32[]{:S(2)}) collective-permute-start(bf16[2,256,512]{2,1,0:T(8,128)(2,1)S(1)} %get-tuple-element.35), channel_id=1, source_target_pairs={{0,5},{1,4},{2,7},{3,6},{4,1},{5,0},{6,3},{7,2},{8,13},{9,12},{10,... | collective-permute-start | bytes 1572872 | tf_op jit(solution)/shard_map/ppermute | solution.py:279
  94.5 4.2 %correlate.4 = (bf16[2,256,512]{2,1,0:T(8,128)(2,1)}, bf16[2,256,512]{2,1,0:T(8,128)(2,1)}, bf16[2,256,512]{2,1,0:T(8,128)(2,1)}, bf16[2,256,512]{2,1,0:T(8,128)(2,1)}) custom-call(s32[2]{0:T(128)S(1)} %pad_add_fusion.3.at_ref, bf16[256,32,128]{2,1,0:T(8,128)(2,1)S(1)} %all-to-all-done.got_ref), custom_call_target="tpu_custom_call" | custom-call | flops 2147483648 | bytes 4194304 | tf_op jit(solution)/shard_map/correlate/pallas_call | solution.py:221
  99.1 0.9 collective-permute-start.4
  99.9 2.7 %collective-permute-start.5 = (bf16[2,256,512]{2,1,0:T(8,128)(2,1)}, bf16[2,256,512]{2,1,0:T(8,128)(2,1)}, u32[]{:S(2)}, u32[]{:S(2)}) collective-permute-start(bf16[2,256,512]{2,1,0:T(8,128)(2,1)} %get-tuple-element.38), channel_id=1, source_target_pairs={{0,6},{1,7},{2,0},{3,1},{4,2},{5,3},{6,4},{7,5},{8,14},{9,15},{10,... | collective-permute-start | bytes 1572872 | tf_op jit(solution)/shard_map/ppermute | solution.py:279
  102.6 3.2 %correlate.5 = (bf16[2,256,512]{2,1,0:T(8,128)(2,1)S(1)}, bf16[2,256,512]{2,1,0:T(8,128)(2,1)}) custom-call(s32[2]{0:T(128)S(1)} %pad_add_fusion.3.at_ref, bf16[256,32,128]{2,1,0:T(8,128)(2,1)S(1)} %all-to-all-done.got_ref), custom_call_target="tpu_custom_call" | custom-call | flops 1073741824 | bytes 3145728 | tf_op jit(solution)/shard_map/correlate/pallas_call | solution.py:221
  105.8 0.8 copy-done.3
  106.6 22.9 %collective-permute-done.1.refs_1_ = bf16[2,256,512]{2,1,0:T(8,128)(2,1)S(1)} collective-permute-done((bf16[2,256,512]{2,1,0:T(8,128)(2,1)S(1)}, bf16[2,256,512]{2,1,0:T(8,128)(2,1)S(1)}, u32[]{:S(2)}, u32[]{:S(2)}) %collective-permute-start.1) | collective-permute-done | bytes 524320 | tf_op jit(solution)/shard_map/ppermute | solution.py:279
  129.5 0.8 copy-done.1
  130.8 1.0 copy-done.2
  131.8 1.0 copy-done.4
  132.9 2.3 %widen.3.refs_0_ = f32[8,2,256,512]{3,2,1,0:T(8,128)} custom-call(s32[3]{0:T(128)S(1)} %pad_add_fusion.2.where_ref, bf16[2,256,512]{2,1,0:T(8,128)(2,1)S(1)} %copy-done.4, bf16[2,256,512]{2,1,0:T(8,128)(2,1)S(1)} %collective-permute-done.1.refs_1_, bf16[2,256,512]{2,1,0:T(8,128)(2,1)S(1)} %copy-done.2), custom_call_target="tpu_custom_call" | custom-call | flops 786432 | bytes 4718592 | tf_op jit(solution)/shard_map/widen/pallas_call | solution.py:248
  135.2 5.4 %collective-permute-done.3.refs_1_ = bf16[2,256,512]{2,1,0:T(8,128)(2,1)S(1)} collective-permute-done((bf16[2,256,512]{2,1,0:T(8,128)(2,1)}, bf16[2,256,512]{2,1,0:T(8,128)(2,1)S(1)}, u32[]{:S(2)}, u32[]{:S(2)}) %collective-permute-start.3) | collective-permute-done | bytes 524320 | tf_op jit(solution)/shard_map/ppermute | solution.py:279
  140.6 2.5 %widen.4.refs_0_ = f32[8,2,256,512]{3,2,1,0:T(8,128)} custom-call(s32[2]{0:T(128)S(1)} %pad_add_fusion.1.where_ref, f32[8,2,256,512]{3,2,1,0:T(8,128)} %widen.3.refs_0_, bf16[2,256,512]{2,1,0:T(8,128)(2,1)S(1)} %collective-permute-done.3.refs_1_, bf16[2,256,512]{2,1,0:T(8,128)(2,1)} %collective-permute-done.4.refs_2_), custom_call_target="tpu_custom_call", output_to_operand_aliasing={{}: (1, {})} | custom-call | flops 524288 | bytes 3145728 | tf_op jit(solution)/shard_map/widen/pallas_call | solution.py:248
  143.6 9.5 %collective-permute-done.7.refs_3_ = bf16[2,256,512]{2,1,0:T(8,128)(2,1)S(1)} collective-permute-done((bf16[2,256,512]{2,1,0:T(8,128)(2,1)}, bf16[2,256,512]{2,1,0:T(8,128)(2,1)S(1)}, u32[]{:S(2)}, u32[]{:S(2)}) %collective-permute-start.7) | collective-permute-done | bytes 524320 | tf_op jit(solution)/shard_map/ppermute | solution.py:279
  153.1 2.8 %widen.5 = f32[8,2,256,512]{3,2,1,0:T(8,128)} custom-call(s32[3]{0:T(128)S(1)} %pad_add_fusion.where_ref, f32[8,2,256,512]{3,2,1,0:T(8,128)} %widen.4.refs_0_, bf16[2,256,512]{2,1,0:T(8,128)(2,1)} %collective-permute-done.5.refs_1_, bf16[2,256,512]{2,1,0:T(8,128)(2,1)S(1)} %collective-permute-done.6.refs_2_, ...), custom_call_target="tpu_custom_call", output_to_operand_aliasing={{}: (1, {})} | custom-call | flops 786432 | bytes 4718592 | tf_op jit(solution)/shard_map/widen/pallas_call | solution.py:248
  (22 shorter events, 2.2 us)
Async XLA Ops:
  0.0 10.3 %copy-start.5 = (bf16[512,512]{1,0:T(8,128)(2,1)S(1)}, bf16[512,512]{1,0:T(8,128)(2,1)}, u32[]{:S(2)}) copy-start(bf16[512,512]{1,0:T(8,128)(2,1)} %constant.82.clone.tab_ref) | copy-start | bytes 1572868
  1.0 9.3 %collective-permute-start = (bf16[32,3584]{1,0:T(8,128)(2,1)S(1)}, bf16[32,3584]{1,0:T(8,128)(2,1)S(1)}, u32[]{:S(2)}, u32[]{:S(2)}) collective-permute-start(bf16[32,3584]{1,0:T(8,128)(2,1)S(1)} %slice.7), channel_id=1, source_target_pairs={{0,1},{1,2},{2,3},{3,4},{4,5},{5,6},{6,7},{8,9},{9,10},{10,11},{11... | collective-permute-start | bytes 688136 | tf_op jit(solution)/shard_map/ppermute | solution.py:268
  6.0 1.6 %copy-start = (bf16[32,32768]{1,0:T(8,128)(2,1)S(1)}, bf16[32,32768]{1,0:T(8,128)(2,1)}, u32[]{:S(2)}) copy-start(bf16[32,32768]{1,0:T(8,128)(2,1)} %v_ref.1) | copy-start | bytes 6291460
  7.6 0.7 copy-start.6
  17.6 71.5 %all-to-all-start = ((bf16[256,32,128]{2,1,0:T(8,128)(2,1)}), bf16[256,32,128]{2,1,0:T(8,128)(2,1)S(1)}, u32[]{:S(2)}, u32[]{:S(2)}) async-start(bf16[256,32,128]{2,1,0:T(8,128)(2,1)} %head_dft.1), calls=%async_computation | async-start | bytes 4194304 | tf_op jit(solution)/shard_map/all_to_all | solution.py:275
  91.4 38.1 %collective-permute-start.1 = (bf16[2,256,512]{2,1,0:T(8,128)(2,1)S(1)}, bf16[2,256,512]{2,1,0:T(8,128)(2,1)S(1)}, u32[]{:S(2)}, u32[]{:S(2)}) collective-permute-start(bf16[2,256,512]{2,1,0:T(8,128)(2,1)S(1)} %get-tuple-element.34), channel_id=1, source_target_pairs={{0,4},{1,5},{2,6},{3,7},{4,0},{5,1},{6,2},{7,3},{8,12},{9,13},{10,... | collective-permute-start | bytes 1572872 | tf_op jit(solution)/shard_map/ppermute | solution.py:279
  91.5 38.0 %collective-permute-start.2 = (bf16[2,256,512]{2,1,0:T(8,128)(2,1)S(1)}, bf16[2,256,512]{2,1,0:T(8,128)(2,1)S(1)}, u32[]{:S(2)}, u32[]{:S(2)}) collective-permute-start(bf16[2,256,512]{2,1,0:T(8,128)(2,1)S(1)} %get-tuple-element.35), channel_id=1, source_target_pairs={{0,5},{1,4},{2,7},{3,6},{4,1},{5,0},{6,3},{7,2},{8,13},{9,12},{10,... | collective-permute-start | bytes 1572872 | tf_op jit(solution)/shard_map/ppermute | solution.py:279
  98.7 41.9 %collective-permute-start.3 = (bf16[2,256,512]{2,1,0:T(8,128)(2,1)}, bf16[2,256,512]{2,1,0:T(8,128)(2,1)S(1)}, u32[]{:S(2)}, u32[]{:S(2)}) collective-permute-start(bf16[2,256,512]{2,1,0:T(8,128)(2,1)} %get-tuple-element.36), channel_id=1, source_target_pairs={{0,2},{1,3},{2,4},{3,5},{4,6},{5,7},{6,0},{7,1},{8,10},{9,11},{10,... | collective-permute-start | bytes 1572872 | tf_op jit(solution)/shard_map/ppermute | solution.py:279
  99.1 41.5 %collective-permute-start.4 = (bf16[2,256,512]{2,1,0:T(8,128)(2,1)}, bf16[2,256,512]{2,1,0:T(8,128)(2,1)}, u32[]{:S(2)}, u32[]{:S(2)}) collective-permute-start(bf16[2,256,512]{2,1,0:T(8,128)(2,1)} %get-tuple-element.37), channel_id=1, source_target_pairs={{0,3},{1,2},{2,5},{3,4},{4,7},{5,6},{6,1},{7,0},{8,11},{9,10},{10,... | collective-permute-start | bytes 1572872 | tf_op jit(solution)/shard_map/ppermute | solution.py:279
  99.9 43.1 %collective-permute-start.5 = (bf16[2,256,512]{2,1,0:T(8,128)(2,1)}, bf16[2,256,512]{2,1,0:T(8,128)(2,1)}, u32[]{:S(2)}, u32[]{:S(2)}) collective-permute-start(bf16[2,256,512]{2,1,0:T(8,128)(2,1)} %get-tuple-element.38), channel_id=1, source_target_pairs={{0,6},{1,7},{2,0},{3,1},{4,2},{5,3},{6,4},{7,5},{8,14},{9,15},{10,... | collective-permute-start | bytes 1572872 | tf_op jit(solution)/shard_map/ppermute | solution.py:279
  105.8 0.8 copy-start.3
  129.5 14.0 %collective-permute-start.6 = (bf16[2,256,512]{2,1,0:T(8,128)(2,1)}, bf16[2,256,512]{2,1,0:T(8,128)(2,1)S(1)}, u32[]{:S(2)}, u32[]{:S(2)}) collective-permute-start(bf16[2,256,512]{2,1,0:T(8,128)(2,1)} %get-tuple-element.39), channel_id=1, source_target_pairs={{0,7},{1,6},{2,1},{3,0},{4,3},{5,2},{6,5},{7,4},{8,15},{9,14},{10,... | collective-permute-start | bytes 1572872 | tf_op jit(solution)/shard_map/ppermute | solution.py:279
  129.5 0.8 copy-start.1
  130.3 22.8 %collective-permute-start.7 = (bf16[2,256,512]{2,1,0:T(8,128)(2,1)}, bf16[2,256,512]{2,1,0:T(8,128)(2,1)S(1)}, u32[]{:S(2)}, u32[]{:S(2)}) collective-permute-start(bf16[2,256,512]{2,1,0:T(8,128)(2,1)} %get-tuple-element.40), channel_id=1, source_target_pairs={{0,1},{1,0},{2,3},{3,2},{4,5},{5,4},{6,7},{7,6},{8,9},{9,8},{10,11... | collective-permute-start | bytes 1572872 | tf_op jit(solution)/shard_map/ppermute | solution.py:279
  130.8 1.0 copy-start.2
  131.8 1.0 copy-start.4

commit v5 on v4

--- a/solution.py
+++ b/solution.py
@@ -231,14 +231,18 @@
 
 
 def widen_kernel(count, where_ref, *refs):
-    pieces, o_ref, wide_ref, sems = refs[-count - 3 : -3], refs[-3], refs[-2], refs[-1]
-    copies = []
-    for j, piece in enumerate(pieces):
-        wide_ref[j] = piece[...].astype(jnp.float32)
-        copies.append(pltpu.make_async_copy(wide_ref.at[j], o_ref.at[where_ref[j]], sems.at[j]))
-        copies[-1].start()
-    for copy in copies:
-        copy.wait()
+    pieces, (o_ref, narrow_ref, wide_ref, in_sems, out_sems) = refs[-count - 5 : -5], refs[-5:]
+    reads = [pltpu.make_async_copy(piece, narrow_ref.at[j], in_sems.at[j]) for j, piece in enumerate(pieces)]
+    for read in reads:
+        read.start()
+    writes = []
+    for j, read in enumerate(reads):
+        read.wait()
+        wide_ref[j] = narrow_ref[j].astype(jnp.float32)
+        writes.append(pltpu.make_async_copy(wide_ref.at[j], o_ref.at[where_ref[j]], out_sems.at[j]))
+        writes[-1].start()
+    for write in writes:
+        write.wait()
 
 
 def widen(pieces, where, shape, into=None):
@@ -247,10 +251,15 @@
     anywhere = pl.BlockSpec(memory_space=pl.ANY)
     return pl.pallas_call(
         functools.partial(widen_kernel, count),
-        in_specs=[SMEM] + [anywhere] * len(before) + [VMEM] * count,
+        in_specs=[SMEM] + [anywhere] * (len(before) + count),
         out_specs=anywhere,
         out_shape=jax.ShapeDtypeStruct(shape, jnp.float32),
-        scratch_shapes=[pltpu.VMEM((count, *piece.shape), jnp.float32), pltpu.SemaphoreType.DMA((count,))],
+        scratch_shapes=[
+            pltpu.VMEM((count, *piece.shape), piece.dtype),
+            pltpu.VMEM((count, *piece.shape), jnp.float32),
+            pltpu.SemaphoreType.DMA((count,)),
+            pltpu.SemaphoreType.DMA((count,)),
+        ],
         input_output_aliases={1: 0} if before else {},
         compiler_params=params(8),
         cost_estimate=cost(count * piece.size, 6 * count * piece.size),
@@ -279,7 +288,7 @@
         return piece if dy == d == 0 else lax.ppermute(piece, ("row", "col"), links)
 
     arrived = []
-    for shifts in ((2,), (1, 3), (0,)):
+    for shifts in ((1,), (3,), (0, 2)):
         sent = correlate(at, turned, groups, rows, cols, shifts, scale)
         turned, sent = lax.optimization_barrier((turned, sent))
         for n, dy in enumerate(shifts):
@@ -287,7 +296,7 @@
                 channel = (row + rows - dy) % rows * cols + (col + cols - d) % cols
                 arrived.append((travel(sent[n * cols + d], dy, d), channel))
     out = None
-    for batch in ((6, 0, 1), (2, 3), (4, 5, 7)):
+    for batch in ((0, 1, 4), (2, 3, 5), (6, 7)):
         where = jnp.stack([arrived[b][1] for b in batch]).astype(jnp.int32)
         out = widen([arrived[b][0] for b in batch], where, shape, out)
     return out

time: 157 us -> 149 us (0.949)
  waiting for transfers between devices: 93.3 us -> 86.2 us
  local copies, waits for them, and re-layouts: 7.96 us -> 6.12 us
    ppermute x7, waiting for transfers between devices: 38.4 us -> 31.3 us  [travel(): return piece if dy == d == 0 else lax.ppermute(piece, ('row', 'col'), links)]
    unnamed x14 -> x10, local copies, waits for them, and re-layouts: 5.98 us -> 4.14 us
  transfers between devices with their start and end apart: 9 -> 9, of which waited for: 5 -> 3; matrix products, arithmetic and copies ran while one was open for 1% -> 1% of each run, Pallas kernels for 9% -> 10%
where the time goes in v5:
time: 149 us
  waiting for transfers between devices  86.2 us (58%)
  starting transfers between devices  28.9 us (19%)
  Pallas kernels  26.9 us (18%)
  local copies, waits for them, and re-layouts  6.12 us (4%)
    all_to_all x1, waiting for transfers between devices, per_device(): lax.all_to_all(message, ALL, split_axis=0, concat_axis=0, tiled=True)  54.9 us
    ppermute x7, waiting for transfers between devices, travel(): return piece if dy == d == 0 else lax.ppermute(piece, ('row', 'col'), links)  31.3 us
    all_to_all x1, starting transfers between devices, per_device(): lax.all_to_all(message, ALL, split_axis=0, concat_axis=0, tiled=True)  16.5 us
    pallas_call x3, Pallas kernels, correlate(): pl.pallas_call(functools.partial(correlate_kernel, groups, rows, cols, sh...  9.79 us
    ppermute x7, starting transfers between devices, travel(): return piece if dy == d == 0 else lax.ppermute(piece, ('row', 'col'), links)  8.49 us
    pallas_call x3, Pallas kernels, widen(): pl.pallas_call(functools.partial(widen_kernel, count), in_specs=[SMEM] +...  7.83 us
    pallas_call x1, Pallas kernels, channelize(): pl.pallas_call(head_kernel, out_shape=jax.ShapeDtypeStruct((CHANNELS, inp...  7.24 us
    unnamed x10, local copies, waits for them, and re-layouts  4.14 us
  transfers between devices with their start and end apart: 9, of which 3 were waited for; matrix products, arithmetic and copies ran while one was open for 1% of the time, Pallas kernels for 10%

profile of v5, /device:TPU:1, one launch (start us, length us, event | category | flops | bytes accessed | tf_op | source)
XLA Modules:
  0.0 148.6 jit_solution(18050437030740554357)
XLA Ops:
  0.0 1.0 slice.7
  1.0 4.0 %collective-permute-start = (bf16[32,3584]{1,0:T(8,128)(2,1)S(1)}, bf16[32,3584]{1,0:T(8,128)(2,1)S(1)}, u32[]{:S(2)}, u32[]{:S(2)}) collective-permute-start(bf16[32,3584]{1,0:T(8,128)(2,1)S(1)} %slice.7), channel_id=1, source_target_pairs={{0,1},{1,2},{2,3},{3,4},{4,5},{5,6},{6,7},{8,9},{9,10},{10,11},{11... | collective-permute-start | bytes 688136 | tf_op jit(solution)/shard_map/ppermute | solution.py:277
  5.0 1.0 slice.6.v_ref
  6.0 1.6 %copy-done = bf16[32,32768]{1,0:T(8,128)(2,1)S(1)} copy-done((bf16[32,32768]{1,0:T(8,128)(2,1)S(1)}, bf16[32,32768]{1,0:T(8,128)(2,1)}, u32[]{:S(2)}) %copy-start) | copy-done | bytes 2097176
  7.6 0.7 copy-done.4
  8.3 2.0 %fir.1.f_ref = f32[4,1792,128]{2,1,0:T(8,128)S(1)} custom-call(bf16[32,32768]{1,0:T(8,128)(2,1)S(1)} %copy-done, f32[8,512]{1,0:T(8,128)S(1)} %copy-done.4), custom_call_target="tpu_custom_call" | custom-call | flops 16777216 | bytes 6291456 | tf_op jit(solution)/shard_map/fir/pallas_call | solution.py:157
  10.3 7.2 %head_dft.1 = bf16[256,32,128]{2,1,0:T(8,128)(2,1)} custom-call(bf16[32,4096]{1,0:T(8,128)(2,1)S(1)} %slice.6.v_ref, bf16[32,3584]{1,0:T(8,128)(2,1)S(1)} %collective-permute-done.h_ref, f32[4,1792,128]{2,1,0:T(8,128)S(1)} %fir.1.f_ref, f32[8,512]{1,0:T(8,128)S(1)} %copy-done.4, bf16[512,512]{1,0:T(8,128)(2,1)S(1)} %copy-done.3), custom_call_target="tpu_custom_call" | custom-call | flops 1073741824 | bytes 6291456 | tf_op jit(solution)/shard_map/head_dft/pallas_call | solution.py:166
  17.6 16.5 %all-to-all-start = ((bf16[256,32,128]{2,1,0:T(8,128)(2,1)}), bf16[256,32,128]{2,1,0:T(8,128)(2,1)S(1)}, u32[]{:S(2)}, u32[]{:S(2)}) async-start(bf16[256,32,128]{2,1,0:T(8,128)(2,1)} %head_dft.1), calls=%async_computation | async-start | bytes 4194304 | tf_op jit(solution)/shard_map/all_to_all | solution.py:284
  34.1 54.9 %all-to-all-done.got_ref = bf16[256,32,128]{2,1,0:T(8,128)(2,1)S(1)} async-done(((bf16[256,32,128]{2,1,0:T(8,128)(2,1)}), bf16[256,32,128]{2,1,0:T(8,128)(2,1)S(1)}, u32[]{:S(2)}, u32[]{:S(2)}) %all-to-all-start) | async-done | bytes 2097184 | tf_op jit(solution)/shard_map/all_to_all | solution.py:284
  89.0 2.4 %correlate.3 = (bf16[2,256,512]{2,1,0:T(8,128)(2,1)S(1)}, bf16[2,256,512]{2,1,0:T(8,128)(2,1)S(1)}) custom-call(s32[2]{0:T(128)S(1)} %pad_add_fusion.3.at_ref, bf16[256,32,128]{2,1,0:T(8,128)(2,1)S(1)} %all-to-all-done.got_ref), custom_call_target="tpu_custom_call" | custom-call | flops 1073741824 | bytes 3145728 | tf_op jit(solution)/shard_map/correlate/pallas_call | solution.py:221
  91.4 0.4 collective-permute-start.1
  91.9 3.2 %correlate.4 = (bf16[2,256,512]{2,1,0:T(8,128)(2,1)}, bf16[2,256,512]{2,1,0:T(8,128)(2,1)}) custom-call(s32[2]{0:T(128)S(1)} %pad_add_fusion.3.at_ref, bf16[256,32,128]{2,1,0:T(8,128)(2,1)S(1)} %all-to-all-done.got_ref), custom_call_target="tpu_custom_call" | custom-call | flops 1073741824 | bytes 3145728 | tf_op jit(solution)/shard_map/correlate/pallas_call | solution.py:221
  95.1 2.6 %collective-permute-start.3 = (bf16[2,256,512]{2,1,0:T(8,128)(2,1)}, bf16[2,256,512]{2,1,0:T(8,128)(2,1)}, u32[]{:S(2)}, u32[]{:S(2)}) collective-permute-start(bf16[2,256,512]{2,1,0:T(8,128)(2,1)} %get-tuple-element.36), channel_id=1, source_target_pairs={{0,6},{1,7},{2,0},{3,1},{4,2},{5,3},{6,4},{7,5},{8,14},{9,15},{10,... | collective-permute-start | bytes 1572872 | tf_op jit(solution)/shard_map/ppermute | solution.py:288
  97.7 2.0 %collective-permute-start.4 = (bf16[2,256,512]{2,1,0:T(8,128)(2,1)}, bf16[2,256,512]{2,1,0:T(8,128)(2,1)}, u32[]{:S(2)}, u32[]{:S(2)}) collective-permute-start(bf16[2,256,512]{2,1,0:T(8,128)(2,1)} %get-tuple-element.37), channel_id=1, source_target_pairs={{0,7},{1,6},{2,1},{3,0},{4,3},{5,2},{6,5},{7,4},{8,15},{9,14},{10,... | collective-permute-start | bytes 1572872 | tf_op jit(solution)/shard_map/ppermute | solution.py:288
  99.7 4.3 %correlate.5 = (bf16[2,256,512]{2,1,0:T(8,128)(2,1)S(1)}, bf16[2,256,512]{2,1,0:T(8,128)(2,1)}, bf16[2,256,512]{2,1,0:T(8,128)(2,1)}, bf16[2,256,512]{2,1,0:T(8,128)(2,1)}) custom-call(s32[2]{0:T(128)S(1)} %pad_add_fusion.3.at_ref, bf16[256,32,128]{2,1,0:T(8,128)(2,1)S(1)} %all-to-all-done.got_ref), custom_call_target="tpu_custom_call" | custom-call | flops 2147483648 | bytes 4194304 | tf_op jit(solution)/shard_map/correlate/pallas_call | solution.py:221
  103.9 0.8 copy-done.1
  104.7 0.3 collective-permute-start.5
  105.0 12.7 %collective-permute-done.1.refs_0_ = bf16[2,256,512]{2,1,0:T(8,128)(2,1)S(1)} collective-permute-done((bf16[2,256,512]{2,1,0:T(8,128)(2,1)S(1)}, bf16[2,256,512]{2,1,0:T(8,128)(2,1)S(1)}, u32[]{:S(2)}, u32[]{:S(2)}) %collective-permute-start.1) | collective-permute-done | bytes 524320 | tf_op jit(solution)/shard_map/ppermute | solution.py:288
  117.8 3.1 %collective-permute-start.7 = (bf16[2,256,512]{2,1,0:T(8,128)(2,1)}, bf16[2,256,512]{2,1,0:T(8,128)(2,1)S(1)}, u32[]{:S(2)}, u32[]{:S(2)}) collective-permute-start(bf16[2,256,512]{2,1,0:T(8,128)(2,1)} %get-tuple-element.40), channel_id=1, source_target_pairs={{0,5},{1,4},{2,7},{3,6},{4,1},{5,0},{6,3},{7,2},{8,13},{9,12},{10,... | collective-permute-start | bytes 1572872 | tf_op jit(solution)/shard_map/ppermute | solution.py:288
  121.1 1.0 copy-done.2
  122.1 2.4 %widen.3.refs_0_ = f32[8,2,256,512]{3,2,1,0:T(8,128)} custom-call(s32[3]{0:T(128)S(1)} %pad_add_fusion.2.where_ref, bf16[2,256,512]{2,1,0:T(8,128)(2,1)S(1)} %collective-permute-done.1.refs_0_, bf16[2,256,512]{2,1,0:T(8,128)(2,1)S(1)} %collective-permute-done.2.refs_1_, bf16[2,256,512]{2,1,0:T(8,128)(2,1)S(1)} %copy-done.2), custom_call_target="tpu_custom_call" | custom-call | flops 786432 | bytes 4718592 | tf_op jit(solution)/shard_map/widen/pallas_call | solution.py:252
  124.5 18.6 %collective-permute-done.3.refs_1_ = bf16[2,256,512]{2,1,0:T(8,128)(2,1)} collective-permute-done((bf16[2,256,512]{2,1,0:T(8,128)(2,1)}, bf16[2,256,512]{2,1,0:T(8,128)(2,1)}, u32[]{:S(2)}, u32[]{:S(2)}) %collective-permute-start.3) | collective-permute-done | bytes 524320 | tf_op jit(solution)/shard_map/ppermute | solution.py:288
  143.1 3.4 %widen.4.refs_0_ = f32[8,2,256,512]{3,2,1,0:T(8,128)} custom-call(s32[3]{0:T(128)S(1)} %pad_add_fusion.1.where_ref, f32[8,2,256,512]{3,2,1,0:T(8,128)} %widen.3.refs_0_, bf16[2,256,512]{2,1,0:T(8,128)(2,1)} %collective-permute-done.3.refs_1_, bf16[2,256,512]{2,1,0:T(8,128)(2,1)} %collective-permute-done.4.refs_2_, ...), custom_call_target="tpu_custom_call", output_to_operand_aliasing={{}: (1, {})} | custom-call | flops 786432 | bytes 4718592 | tf_op jit(solution)/shard_map/widen/pallas_call | solution.py:252
  146.5 2.0 %widen.5 = f32[8,2,256,512]{3,2,1,0:T(8,128)} custom-call(s32[2]{0:T(128)S(1)} %pad_add_fusion.where_ref, f32[8,2,256,512]{3,2,1,0:T(8,128)} %widen.4.refs_0_, bf16[2,256,512]{2,1,0:T(8,128)(2,1)S(1)} %collective-permute-done.6.refs_1_, bf16[2,256,512]{2,1,0:T(8,128)(2,1)S(1)} %collective-permute-done.7.refs_2_), custom_call_target="tpu_custom_call", output_to_operand_aliasing={{}: (1, {})} | custom-call | flops 524288 | bytes 3145728 | tf_op jit(solution)/shard_map/widen/pallas_call | solution.py:252
  (18 shorter events, 0.4 us)
Async XLA Ops:
  0.0 10.3 %copy-start.3 = (bf16[512,512]{1,0:T(8,128)(2,1)S(1)}, bf16[512,512]{1,0:T(8,128)(2,1)}, u32[]{:S(2)}) copy-start(bf16[512,512]{1,0:T(8,128)(2,1)} %constant.82.clone.tab_ref) | copy-start | bytes 1572868
  1.0 9.3 %collective-permute-start = (bf16[32,3584]{1,0:T(8,128)(2,1)S(1)}, bf16[32,3584]{1,0:T(8,128)(2,1)S(1)}, u32[]{:S(2)}, u32[]{:S(2)}) collective-permute-start(bf16[32,3584]{1,0:T(8,128)(2,1)S(1)} %slice.7), channel_id=1, source_target_pairs={{0,1},{1,2},{2,3},{3,4},{4,5},{5,6},{6,7},{8,9},{9,10},{10,11},{11... | collective-permute-start | bytes 688136 | tf_op jit(solution)/shard_map/ppermute | solution.py:277
  6.0 1.6 %copy-start = (bf16[32,32768]{1,0:T(8,128)(2,1)S(1)}, bf16[32,32768]{1,0:T(8,128)(2,1)}, u32[]{:S(2)}) copy-start(bf16[32,32768]{1,0:T(8,128)(2,1)} %v_ref.1) | copy-start | bytes 6291460
  7.6 0.7 copy-start.4
  17.6 71.5 %all-to-all-start = ((bf16[256,32,128]{2,1,0:T(8,128)(2,1)}), bf16[256,32,128]{2,1,0:T(8,128)(2,1)S(1)}, u32[]{:S(2)}, u32[]{:S(2)}) async-start(bf16[256,32,128]{2,1,0:T(8,128)(2,1)} %head_dft.1), calls=%async_computation | async-start | bytes 4194304 | tf_op jit(solution)/shard_map/all_to_all | solution.py:284
  91.4 26.4 %collective-permute-start.1 = (bf16[2,256,512]{2,1,0:T(8,128)(2,1)S(1)}, bf16[2,256,512]{2,1,0:T(8,128)(2,1)S(1)}, u32[]{:S(2)}, u32[]{:S(2)}) collective-permute-start(bf16[2,256,512]{2,1,0:T(8,128)(2,1)S(1)} %get-tuple-element.25), channel_id=1, source_target_pairs={{0,2},{1,3},{2,4},{3,5},{4,6},{5,7},{6,0},{7,1},{8,10},{9,11},{10,... | collective-permute-start | bytes 1572872 | tf_op jit(solution)/shard_map/ppermute | solution.py:288
  91.8 26.0 %collective-permute-start.2 = (bf16[2,256,512]{2,1,0:T(8,128)(2,1)S(1)}, bf16[2,256,512]{2,1,0:T(8,128)(2,1)S(1)}, u32[]{:S(2)}, u32[]{:S(2)}) collective-permute-start(bf16[2,256,512]{2,1,0:T(8,128)(2,1)S(1)} %get-tuple-element.26), channel_id=1, source_target_pairs={{0,3},{1,2},{2,5},{3,4},{4,7},{5,6},{6,1},{7,0},{8,11},{9,10},{10,... | collective-permute-start | bytes 1572872 | tf_op jit(solution)/shard_map/ppermute | solution.py:288
  95.1 48.0 %collective-permute-start.3 = (bf16[2,256,512]{2,1,0:T(8,128)(2,1)}, bf16[2,256,512]{2,1,0:T(8,128)(2,1)}, u32[]{:S(2)}, u32[]{:S(2)}) collective-permute-start(bf16[2,256,512]{2,1,0:T(8,128)(2,1)} %get-tuple-element.36), channel_id=1, source_target_pairs={{0,6},{1,7},{2,0},{3,1},{4,2},{5,3},{6,4},{7,5},{8,14},{9,15},{10,... | collective-permute-start | bytes 1572872 | tf_op jit(solution)/shard_map/ppermute | solution.py:288
  97.7 45.5 %collective-permute-start.4 = (bf16[2,256,512]{2,1,0:T(8,128)(2,1)}, bf16[2,256,512]{2,1,0:T(8,128)(2,1)}, u32[]{:S(2)}, u32[]{:S(2)}) collective-permute-start(bf16[2,256,512]{2,1,0:T(8,128)(2,1)} %get-tuple-element.37), channel_id=1, source_target_pairs={{0,7},{1,6},{2,1},{3,0},{4,3},{5,2},{6,5},{7,4},{8,15},{9,14},{10,... | collective-permute-start | bytes 1572872 | tf_op jit(solution)/shard_map/ppermute | solution.py:288
  103.9 0.8 copy-start.1
  104.7 38.4 %collective-permute-start.5 = (bf16[2,256,512]{2,1,0:T(8,128)(2,1)}, bf16[2,256,512]{2,1,0:T(8,128)(2,1)S(1)}, u32[]{:S(2)}, u32[]{:S(2)}) collective-permute-start(bf16[2,256,512]{2,1,0:T(8,128)(2,1)} %get-tuple-element.38), channel_id=1, source_target_pairs={{0,1},{1,0},{2,3},{3,2},{4,5},{5,4},{6,7},{7,6},{8,9},{9,8},{10,11... | collective-permute-start | bytes 1572872 | tf_op jit(solution)/shard_map/ppermute | solution.py:288
  117.8 28.7 %collective-permute-start.6 = (bf16[2,256,512]{2,1,0:T(8,128)(2,1)}, bf16[2,256,512]{2,1,0:T(8,128)(2,1)S(1)}, u32[]{:S(2)}, u32[]{:S(2)}) collective-permute-start(bf16[2,256,512]{2,1,0:T(8,128)(2,1)} %get-tuple-element.39), channel_id=1, source_target_pairs={{0,4},{1,5},{2,6},{3,7},{4,0},{5,1},{6,2},{7,3},{8,12},{9,13},{10,... | collective-permute-start | bytes 1572872 | tf_op jit(solution)/shard_map/ppermute | solution.py:288
  117.8 28.7 %collective-permute-start.7 = (bf16[2,256,512]{2,1,0:T(8,128)(2,1)}, bf16[2,256,512]{2,1,0:T(8,128)(2,1)S(1)}, u32[]{:S(2)}, u32[]{:S(2)}) collective-permute-start(bf16[2,256,512]{2,1,0:T(8,128)(2,1)} %get-tuple-element.40), channel_id=1, source_target_pairs={{0,5},{1,4},{2,7},{3,6},{4,1},{5,0},{6,3},{7,2},{8,13},{9,12},{10,... | collective-permute-start | bytes 1572872 | tf_op jit(solution)/shard_map/ppermute | solution.py:288
  121.1 1.0 copy-start.2

commit v6 on v5

--- a/solution.py
+++ b/solution.py
@@ -112,7 +112,7 @@
             t_ref[pl.ds(row + 1, channels, stride=inputs), :] = odd
         return carry
 
-    lax.fori_loop(0, inputs // group, transform, 0)
+    lax.fori_loop(0, inputs // group, transform, 0, unroll=True)
 
     step = 8
 
@@ -122,7 +122,7 @@
             o_ref[index * step + j] = t_ref[pl.ds(first, inputs), :].astype(jnp.bfloat16)
         return carry
 
-    lax.fori_loop(0, channels // step, cast, 0)
+    lax.fori_loop(0, channels // step, cast, 0, unroll=4)
 
 
 def head_kernel(v_ref, h_ref, f_ref, w_ref, tab_ref, o_ref, head_ref, t_ref):
@@ -296,7 +296,7 @@
                 channel = (row + rows - dy) % rows * cols + (col + cols - d) % cols
                 arrived.append((travel(sent[n * cols + d], dy, d), channel))
     out = None
-    for batch in ((0, 1, 4), (2, 3, 5), (6, 7)):
+    for batch in ((0, 1, 4), (2, 3, 5), (6,), (7,)):
         where = jnp.stack([arrived[b][1] for b in batch]).astype(jnp.int32)
         out = widen([arrived[b][0] for b in batch], where, shape, out)
     return out

time: 149 us -> 149 us (level)
    pallas_call x3 -> x4, Pallas kernels: 7.83 us -> 7.99 us  [widen(): pl.pallas_call(functools.partial(widen_kernel, count), in_specs=[SMEM] +...]
  transfers between devices with their start and end apart: 9 -> 9, of which waited for: 3 -> 3; matrix products, arithmetic and copies ran while one was open for 1% -> 1% of each run, Pallas kernels for 10% -> 11%
where the time goes in v6:
time: 149 us
  waiting for transfers between devices  86.3 us (58%)
  starting transfers between devices  29 us (19%)
  Pallas kernels  25.9 us (17%)
  local copies, waits for them, and re-layouts  7.1 us (5%)
    all_to_all x1, waiting for transfers between devices, per_device(): lax.all_to_all(message, ALL, split_axis=0, concat_axis=0, tiled=True)  54.9 us
    ppermute x7, waiting for transfers between devices, travel(): return piece if dy == d == 0 else lax.ppermute(piece, ('row', 'col'), links)  31.4 us
    all_to_all x1, starting transfers between devices, per_device(): lax.all_to_all(message, ALL, split_axis=0, concat_axis=0, tiled=True)  16.5 us
    pallas_call x3, Pallas kernels, correlate(): pl.pallas_call(functools.partial(correlate_kernel, groups, rows, cols, sh...  9.75 us
    ppermute x7, starting transfers between devices, travel(): return piece if dy == d == 0 else lax.ppermute(piece, ('row', 'col'), links)  8.5 us
    pallas_call x4, Pallas kernels, widen(): pl.pallas_call(functools.partial(widen_kernel, count), in_specs=[SMEM] +...  7.99 us
    pallas_call x1, Pallas kernels, channelize(): pl.pallas_call(head_kernel, out_shape=jax.ShapeDtypeStruct((CHANNELS, inp...  6.14 us
    unnamed x10, local copies, waits for them, and re-layouts  5.18 us
  transfers between devices with their start and end apart: 9, of which 3 were waited for; matrix products, arithmetic and copies ran while one was open for 1% of the time, Pallas kernels for 11%

profile of v6, /device:TPU:1, one launch (start us, length us, event | category | flops | bytes accessed | tf_op | source)
XLA Modules:
  0.0 148.8 jit_solution(9880115403860195733)
XLA Ops:
  0.0 1.0 slice.7
  1.0 4.0 %collective-permute-start = (bf16[32,3584]{1,0:T(8,128)(2,1)S(1)}, bf16[32,3584]{1,0:T(8,128)(2,1)S(1)}, u32[]{:S(2)}, u32[]{:S(2)}) collective-permute-start(bf16[32,3584]{1,0:T(8,128)(2,1)S(1)} %slice.7), channel_id=1, source_target_pairs={{0,1},{1,2},{2,3},{3,4},{4,5},{5,6},{6,7},{8,9},{9,10},{10,11},{11... | collective-permute-start | bytes 688136 | tf_op jit(solution)/shard_map/ppermute | solution.py:277
  4.9 1.0 slice.6.v_ref
  5.9 1.6 %copy-done = bf16[32,32768]{1,0:T(8,128)(2,1)S(1)} copy-done((bf16[32,32768]{1,0:T(8,128)(2,1)S(1)}, bf16[32,32768]{1,0:T(8,128)(2,1)}, u32[]{:S(2)}) %copy-start) | copy-done | bytes 2097176
  7.5 0.7 copy-done.4
  8.2 2.0 %fir.1.f_ref = f32[4,1792,128]{2,1,0:T(8,128)S(1)} custom-call(bf16[32,32768]{1,0:T(8,128)(2,1)S(1)} %copy-done, f32[8,512]{1,0:T(8,128)S(1)} %copy-done.4), custom_call_target="tpu_custom_call" | custom-call | flops 16777216 | bytes 6291456 | tf_op jit(solution)/shard_map/fir/pallas_call | solution.py:157
  10.3 1.0 copy-done.3
  11.3 6.1 %head_dft.1 = bf16[256,32,128]{2,1,0:T(8,128)(2,1)} custom-call(bf16[32,4096]{1,0:T(8,128)(2,1)S(1)} %slice.6.v_ref, bf16[32,3584]{1,0:T(8,128)(2,1)S(1)} %collective-permute-done.h_ref, f32[4,1792,128]{2,1,0:T(8,128)S(1)} %fir.1.f_ref, f32[8,512]{1,0:T(8,128)S(1)} %copy-done.4, bf16[512,512]{1,0:T(8,128)(2,1)S(1)} %copy-done.3), custom_call_target="tpu_custom_call" | custom-call | flops 1073741824 | bytes 6291456 | tf_op jit(solution)/shard_map/head_dft/pallas_call | solution.py:166
  17.4 16.5 %all-to-all-start = ((bf16[256,32,128]{2,1,0:T(8,128)(2,1)}), bf16[256,32,128]{2,1,0:T(8,128)(2,1)S(1)}, u32[]{:S(2)}, u32[]{:S(2)}) async-start(bf16[256,32,128]{2,1,0:T(8,128)(2,1)} %head_dft.1), calls=%async_computation | async-start | bytes 4194304 | tf_op jit(solution)/shard_map/all_to_all | solution.py:284
  34.0 54.9 %all-to-all-done.got_ref = bf16[256,32,128]{2,1,0:T(8,128)(2,1)S(1)} async-done(((bf16[256,32,128]{2,1,0:T(8,128)(2,1)}), bf16[256,32,128]{2,1,0:T(8,128)(2,1)S(1)}, u32[]{:S(2)}, u32[]{:S(2)}) %all-to-all-start) | async-done | bytes 2097184 | tf_op jit(solution)/shard_map/all_to_all | solution.py:284
  88.9 2.4 %correlate.3 = (bf16[2,256,512]{2,1,0:T(8,128)(2,1)S(1)}, bf16[2,256,512]{2,1,0:T(8,128)(2,1)S(1)}) custom-call(s32[2]{0:T(128)S(1)} %pad_add_fusion.2.at_ref, bf16[256,32,128]{2,1,0:T(8,128)(2,1)S(1)} %all-to-all-done.got_ref), custom_call_target="tpu_custom_call" | custom-call | flops 1073741824 | bytes 3145728 | tf_op jit(solution)/shard_map/correlate/pallas_call | solution.py:221
  91.8 3.2 %correlate.4 = (bf16[2,256,512]{2,1,0:T(8,128)(2,1)}, bf16[2,256,512]{2,1,0:T(8,128)(2,1)}) custom-call(s32[2]{0:T(128)S(1)} %pad_add_fusion.2.at_ref, bf16[256,32,128]{2,1,0:T(8,128)(2,1)S(1)} %all-to-all-done.got_ref), custom_call_target="tpu_custom_call" | custom-call | flops 1073741824 | bytes 3145728 | tf_op jit(solution)/shard_map/correlate/pallas_call | solution.py:221
  95.0 2.6 %collective-permute-start.3 = (bf16[2,256,512]{2,1,0:T(8,128)(2,1)}, bf16[2,256,512]{2,1,0:T(8,128)(2,1)}, u32[]{:S(2)}, u32[]{:S(2)}) collective-permute-start(bf16[2,256,512]{2,1,0:T(8,128)(2,1)} %get-tuple-element.36), channel_id=1, source_target_pairs={{0,6},{1,7},{2,0},{3,1},{4,2},{5,3},{6,4},{7,5},{8,14},{9,15},{10,... | collective-permute-start | bytes 1572872 | tf_op jit(solution)/shard_map/ppermute | solution.py:288
  97.6 2.0 %collective-permute-start.4 = (bf16[2,256,512]{2,1,0:T(8,128)(2,1)}, bf16[2,256,512]{2,1,0:T(8,128)(2,1)}, u32[]{:S(2)}, u32[]{:S(2)}) collective-permute-start(bf16[2,256,512]{2,1,0:T(8,128)(2,1)} %get-tuple-element.37), channel_id=1, source_target_pairs={{0,7},{1,6},{2,1},{3,0},{4,3},{5,2},{6,5},{7,4},{8,15},{9,14},{10,... | collective-permute-start | bytes 1572872 | tf_op jit(solution)/shard_map/ppermute | solution.py:288
  99.6 4.2 %correlate.5 = (bf16[2,256,512]{2,1,0:T(8,128)(2,1)S(1)}, bf16[2,256,512]{2,1,0:T(8,128)(2,1)}, bf16[2,256,512]{2,1,0:T(8,128)(2,1)}, bf16[2,256,512]{2,1,0:T(8,128)(2,1)}) custom-call(s32[2]{0:T(128)S(1)} %pad_add_fusion.2.at_ref, bf16[256,32,128]{2,1,0:T(8,128)(2,1)S(1)} %all-to-all-done.got_ref), custom_call_target="tpu_custom_call" | custom-call | flops 2147483648 | bytes 4194304 | tf_op jit(solution)/shard_map/correlate/pallas_call | solution.py:221
  103.8 0.8 copy-done.1
  104.9 12.8 %collective-permute-done.1.refs_0_ = bf16[2,256,512]{2,1,0:T(8,128)(2,1)S(1)} collective-permute-done((bf16[2,256,512]{2,1,0:T(8,128)(2,1)S(1)}, bf16[2,256,512]{2,1,0:T(8,128)(2,1)S(1)}, u32[]{:S(2)}, u32[]{:S(2)}) %collective-permute-start.1) | collective-permute-done | bytes 524320 | tf_op jit(solution)/shard_map/ppermute | solution.py:288
  117.7 3.1 %collective-permute-start.7 = (bf16[2,256,512]{2,1,0:T(8,128)(2,1)}, bf16[2,256,512]{2,1,0:T(8,128)(2,1)S(1)}, u32[]{:S(2)}, u32[]{:S(2)}) collective-permute-start(bf16[2,256,512]{2,1,0:T(8,128)(2,1)} %get-tuple-element.40), channel_id=1, source_target_pairs={{0,5},{1,4},{2,7},{3,6},{4,1},{5,0},{6,3},{7,2},{8,13},{9,12},{10,... | collective-permute-start | bytes 1572872 | tf_op jit(solution)/shard_map/ppermute | solution.py:288
  120.9 1.0 copy-done.2
  121.9 2.4 %widen.4.refs_0_ = f32[8,2,256,512]{3,2,1,0:T(8,128)} custom-call(s32[3]{0:T(128)S(1)} %pad_add_fusion.1.where_ref, bf16[2,256,512]{2,1,0:T(8,128)(2,1)S(1)} %collective-permute-done.1.refs_0_, bf16[2,256,512]{2,1,0:T(8,128)(2,1)S(1)} %collective-permute-done.2.refs_1_, bf16[2,256,512]{2,1,0:T(8,128)(2,1)S(1)} %copy-done.2), custom_call_target="tpu_custom_call" | custom-call | flops 786432 | bytes 4718592 | tf_op jit(solution)/shard_map/widen/pallas_call | solution.py:252
  124.4 18.6 %collective-permute-done.3.refs_1_ = bf16[2,256,512]{2,1,0:T(8,128)(2,1)} collective-permute-done((bf16[2,256,512]{2,1,0:T(8,128)(2,1)}, bf16[2,256,512]{2,1,0:T(8,128)(2,1)}, u32[]{:S(2)}, u32[]{:S(2)}) %collective-permute-start.3) | collective-permute-done | bytes 524320 | tf_op jit(solution)/shard_map/ppermute | solution.py:288
  143.0 3.4 %widen.5.refs_0_ = f32[8,2,256,512]{3,2,1,0:T(8,128)} custom-call(s32[3]{0:T(128)S(1)} %pad_add_fusion.where_ref, f32[8,2,256,512]{3,2,1,0:T(8,128)} %widen.4.refs_0_, bf16[2,256,512]{2,1,0:T(8,128)(2,1)} %collective-permute-done.3.refs_1_, bf16[2,256,512]{2,1,0:T(8,128)(2,1)} %collective-permute-done.4.refs_2_, ...), custom_call_target="tpu_custom_call", output_to_operand_aliasing={{}: (1, {})} | custom-call | flops 786432 | bytes 4718592 | tf_op jit(solution)/shard_map/widen/pallas_call | solution.py:252
  146.4 1.1 widen.6.refs_0_
  147.5 1.1 widen.7
  (18 shorter events, 1.1 us)
Async XLA Ops:
  1.0 9.3 %collective-permute-start = (bf16[32,3584]{1,0:T(8,128)(2,1)S(1)}, bf16[32,3584]{1,0:T(8,128)(2,1)S(1)}, u32[]{:S(2)}, u32[]{:S(2)}) collective-permute-start(bf16[32,3584]{1,0:T(8,128)(2,1)S(1)} %slice.7), channel_id=1, source_target_pairs={{0,1},{1,2},{2,3},{3,4},{4,5},{5,6},{6,7},{8,9},{9,10},{10,11},{11... | collective-permute-start | bytes 688136 | tf_op jit(solution)/shard_map/ppermute | solution.py:277
  5.9 1.6 %copy-start = (bf16[32,32768]{1,0:T(8,128)(2,1)S(1)}, bf16[32,32768]{1,0:T(8,128)(2,1)}, u32[]{:S(2)}) copy-start(bf16[32,32768]{1,0:T(8,128)(2,1)} %v_ref.1) | copy-start | bytes 6291460
  7.5 0.7 copy-start.4
  10.2 1.0 copy-start.3
  17.4 71.5 %all-to-all-start = ((bf16[256,32,128]{2,1,0:T(8,128)(2,1)}), bf16[256,32,128]{2,1,0:T(8,128)(2,1)S(1)}, u32[]{:S(2)}, u32[]{:S(2)}) async-start(bf16[256,32,128]{2,1,0:T(8,128)(2,1)} %head_dft.1), calls=%async_computation | async-start | bytes 4194304 | tf_op jit(solution)/shard_map/all_to_all | solution.py:284
  91.3 26.4 %collective-permute-start.1 = (bf16[2,256,512]{2,1,0:T(8,128)(2,1)S(1)}, bf16[2,256,512]{2,1,0:T(8,128)(2,1)S(1)}, u32[]{:S(2)}, u32[]{:S(2)}) collective-permute-start(bf16[2,256,512]{2,1,0:T(8,128)(2,1)S(1)} %get-tuple-element.25), channel_id=1, source_target_pairs={{0,2},{1,3},{2,4},{3,5},{4,6},{5,7},{6,0},{7,1},{8,10},{9,11},{10,... | collective-permute-start | bytes 1572872 | tf_op jit(solution)/shard_map/ppermute | solution.py:288
  91.7 26.0 %collective-permute-start.2 = (bf16[2,256,512]{2,1,0:T(8,128)(2,1)S(1)}, bf16[2,256,512]{2,1,0:T(8,128)(2,1)S(1)}, u32[]{:S(2)}, u32[]{:S(2)}) collective-permute-start(bf16[2,256,512]{2,1,0:T(8,128)(2,1)S(1)} %get-tuple-element.26), channel_id=1, source_target_pairs={{0,3},{1,2},{2,5},{3,4},{4,7},{5,6},{6,1},{7,0},{8,11},{9,10},{10,... | collective-permute-start | bytes 1572872 | tf_op jit(solution)/shard_map/ppermute | solution.py:288
  95.0 48.0 %collective-permute-start.3 = (bf16[2,256,512]{2,1,0:T(8,128)(2,1)}, bf16[2,256,512]{2,1,0:T(8,128)(2,1)}, u32[]{:S(2)}, u32[]{:S(2)}) collective-permute-start(bf16[2,256,512]{2,1,0:T(8,128)(2,1)} %get-tuple-element.36), channel_id=1, source_target_pairs={{0,6},{1,7},{2,0},{3,1},{4,2},{5,3},{6,4},{7,5},{8,14},{9,15},{10,... | collective-permute-start | bytes 1572872 | tf_op jit(solution)/shard_map/ppermute | solution.py:288
  97.6 45.4 %collective-permute-start.4 = (bf16[2,256,512]{2,1,0:T(8,128)(2,1)}, bf16[2,256,512]{2,1,0:T(8,128)(2,1)}, u32[]{:S(2)}, u32[]{:S(2)}) collective-permute-start(bf16[2,256,512]{2,1,0:T(8,128)(2,1)} %get-tuple-element.37), channel_id=1, source_target_pairs={{0,7},{1,6},{2,1},{3,0},{4,3},{5,2},{6,5},{7,4},{8,15},{9,14},{10,... | collective-permute-start | bytes 1572872 | tf_op jit(solution)/shard_map/ppermute | solution.py:288
  103.8 0.8 copy-start.1
  104.6 38.4 %collective-permute-start.5 = (bf16[2,256,512]{2,1,0:T(8,128)(2,1)}, bf16[2,256,512]{2,1,0:T(8,128)(2,1)S(1)}, u32[]{:S(2)}, u32[]{:S(2)}) collective-permute-start(bf16[2,256,512]{2,1,0:T(8,128)(2,1)} %get-tuple-element.38), channel_id=1, source_target_pairs={{0,1},{1,0},{2,3},{3,2},{4,5},{5,4},{6,7},{7,6},{8,9},{9,8},{10,11... | collective-permute-start | bytes 1572872 | tf_op jit(solution)/shard_map/ppermute | solution.py:288
  117.7 28.7 %collective-permute-start.6 = (bf16[2,256,512]{2,1,0:T(8,128)(2,1)}, bf16[2,256,512]{2,1,0:T(8,128)(2,1)S(1)}, u32[]{:S(2)}, u32[]{:S(2)}) collective-permute-start(bf16[2,256,512]{2,1,0:T(8,128)(2,1)} %get-tuple-element.39), channel_id=1, source_target_pairs={{0,4},{1,5},{2,6},{3,7},{4,0},{5,1},{6,2},{7,3},{8,12},{9,13},{10,... | collective-permute-start | bytes 1572872 | tf_op jit(solution)/shard_map/ppermute | solution.py:288
  117.7 29.8 %collective-permute-start.7 = (bf16[2,256,512]{2,1,0:T(8,128)(2,1)}, bf16[2,256,512]{2,1,0:T(8,128)(2,1)S(1)}, u32[]{:S(2)}, u32[]{:S(2)}) collective-permute-start(bf16[2,256,512]{2,1,0:T(8,128)(2,1)} %get-tuple-element.40), channel_id=1, source_target_pairs={{0,5},{1,4},{2,7},{3,6},{4,1},{5,0},{6,3},{7,2},{8,13},{9,12},{10,... | collective-permute-start | bytes 1572872 | tf_op jit(solution)/shard_map/ppermute | solution.py:288
  120.9 1.0 copy-start.2
